TPU v7x, 512 devices: a whole 4x4x16 slice. The times are simulated.
512 devices in a mesh: row: 16 (over x, y), col: 32 (over z, core).
Axes of the slice: x: 4, y: 4, z: 16, core: 2. Of those that a mesh axis runs over, the one named last changes fastest.
Arguments:
- front: bfloat16 [16384, 16384], P('row', 'col'), may hold values from -0.046875 to 0.046875
- diag_inverse: float32 [128, 128, 128], P('row'), may hold values from -0.25 to 1.5
- load: float32 [8, 16384], P(None, 'row'), may hold values from -6 to 6
- panel_order: int32 [128], replicated, may hold values from 0 to 127, each once
- tie: float32 [32, 16384], P('col', 'row'), may hold values from 0.5 to 1.5
- mass: float32 [32, 16384], P('col', 'row'), may hold values from 0.5 to 6
- modes: bfloat16 [1024, 32, 16384], P(None, 'col', 'row'), may hold values from -0.0234375 to 0.0234375
Outputs:
- front_solution: float32 [8, 16384], P(None, 'row')
- residual_vectors: float32 [8, 32, 16384], P(None, 'col', 'row')
All inputs are finite; a program needn't handle non-finite values.
Results may differ from a plain program's by a relative error of at most 0.0049.
Values may be sent and summed in bfloat16 or wider, within the bound.
No kernel may reach another device: no remote copies, remote signals or barrier semaphores. Data moves between devices by JAX's collectives and lax.ppermute only.
A program may use at most 64 MiB of HBM per device.

v0:
```python
import jax
import jax.numpy as jnp
from jax import lax
from jax.sharding import PartitionSpec as P

LEVELS = 4


highest = lax.Precision.HIGHEST


def on_device(front, diag_inverse, load, panel_order, tie, mass, modes):
    vectors = load.shape[0]
    block_size = diag_inverse.shape[1]
    local_panels = diag_inverse.shape[0]
    rows_local = front.shape[0]
    cols_local = front.shape[1]
    panels = panel_order.shape[0]
    row_at = lax.axis_index("row")
    col_at = lax.axis_index("col")
    counting = jnp.arange(panels, dtype=jnp.int32)
    matches = panel_order[:, None] == counting[None, :]
    ranks = jnp.sum(jnp.where(matches, counting[:, None], 0), axis=0)
    levels_of = ranks // (panels // LEVELS)
    position_level = jnp.repeat(levels_of, block_size)
    row_level = lax.dynamic_slice_in_dim(position_level, row_at * rows_local, rows_local, 0)
    pending = jnp.zeros((vectors, rows_local), jnp.float32)
    forward_out = jnp.zeros((vectors, rows_local), jnp.float32)
    for level in range(LEVELS):
        if level > 0:
            total_sum = lax.psum(pending, "col")
        else:
            total_sum = pending
        remain = (load - total_sum).reshape(vectors, local_panels, block_size)
        candidate = jnp.einsum("vpj,pij->vpi", remain, diag_inverse, precision=highest).reshape(
            vectors, rows_local
        )
        chosen = row_level[None, :] == level
        forward_out = jnp.where(chosen, candidate, forward_out)
        if level < LEVELS - 1:
            fresh = jnp.where(chosen, forward_out, 0.0).astype(jnp.bfloat16)
            whole = lax.all_gather(fresh, "row", axis=1, tiled=True)
            mine = lax.dynamic_slice_in_dim(whole, col_at * cols_local, cols_local, 1)
            pending = pending + jnp.dot(mine, front.T, preferred_element_type=jnp.float32)
    back_pending = jnp.zeros((vectors, cols_local), jnp.float32)
    back_out = jnp.zeros((vectors, rows_local), jnp.float32)
    for level in reversed(range(LEVELS)):
        if level < LEVELS - 1:
            column_sum = lax.psum(back_pending, "row")
            full_sum = lax.all_gather(column_sum, "col", axis=1, tiled=True)
            here = lax.dynamic_slice_in_dim(full_sum, row_at * rows_local, rows_local, 1)
        else:
            here = jnp.zeros((vectors, rows_local), jnp.float32)
        remain = (forward_out - here).reshape(vectors, local_panels, block_size)
        candidate = jnp.einsum("vpj,pji->vpi", remain, diag_inverse, precision=highest).reshape(
            vectors, rows_local
        )
        chosen = row_level[None, :] == level
        back_out = jnp.where(chosen, candidate, back_out)
        if level > 0:
            fresh = jnp.where(chosen, back_out, 0.0).astype(jnp.bfloat16)
            back_pending = back_pending + jnp.dot(fresh, front, preferred_element_type=jnp.float32)
    static = tie[None, :, :] * back_out[:, None, :]
    weighted = (mass[None, :, :] * static).astype(jnp.bfloat16).reshape(vectors, -1)
    mode_rows = modes.reshape(modes.shape[0], -1)
    partial_coords = lax.dot_general(
        weighted, mode_rows, (((1,), (1,)), ((), ())), preferred_element_type=jnp.float32
    )
    coords = lax.psum(partial_coords, ("row", "col"))
    correction = jnp.dot(coords.astype(jnp.bfloat16), mode_rows, preferred_element_type=jnp.float32)
    return (back_out, static - correction.reshape(static.shape))


def solution(mesh):
    in_specs = (
        P("row", "col"),
        P("row", None, None),
        P(None, "row"),
        P(),
        P("col", "row"),
        P("col", "row"),
        P(None, "col", "row"),
    )
    out_specs = (P(None, "row"), P(None, "col", "row"))
    return jax.shard_map(
        on_device, mesh=mesh, in_specs=in_specs, out_specs=out_specs, check_vma=False
    )
```

profile of v0, /device:TPU:1, one launch (start us, length us, event | category | flops | bytes accessed | tf_op | source)
XLA Modules:
  0.0 765.4 jit_solution(5559178636949547583)
XLA Ops:
  0.7 0.9 select_reduce_fusion
  1.7 2.0 select_convert_fusion.5
  3.7 19.7 %all_gather.18 = bf16[8,16384]{1,0:T(8,128)(2,1)S(1)} all-gather(bf16[8,1024]{1,0:T(8,128)(2,1)S(1)} %get-tuple-element.14), channel_id=1, replica_groups=mesh['row'=16,'col'=32] {'row'}, dimensions={1}, use_global_device_ids=true | all-gather | bytes 278528 | tf_op jit(solution)/shard_map/all_gather | solution.py:42
  23.3 1.6 fusion.64
  24.9 99.0 %psum.49 = f32[8,1024]{1,0:T(8,128)S(1)} all-reduce(f32[8,1024]{1,0:T(8,128)S(1)} %fusion.64), channel_id=1, replica_groups=mesh['row'=16,'col'=32] {'col'}, use_global_device_ids=true, to_apply=%region_1.2 | all-reduce | flops 8192 | bytes 65536 | tf_op jit(solution)/shard_map/psum | solution.py:31
  123.9 2.0 select_convert_fusion.4
  125.9 17.9 %all_gather.19 = bf16[8,16384]{1,0:T(8,128)(2,1)S(1)} all-gather(bf16[8,1024]{1,0:T(8,128)(2,1)S(1)} %get-tuple-element.8), channel_id=1, replica_groups=mesh['row'=16,'col'=32] {'row'}, dimensions={1}, use_global_device_ids=true | all-gather | bytes 278528 | tf_op jit(solution)/shard_map/all_gather | solution.py:42
  144.2 95.2 %psum.50 = f32[8,1024]{1,0:T(8,128)S(1)} all-reduce(f32[8,1024]{1,0:T(8,128)S(1)} %convolution_add_fusion.1), channel_id=1, replica_groups=mesh['row'=16,'col'=32] {'col'}, use_global_device_ids=true, to_apply=%region_2.3 | all-reduce | flops 8192 | bytes 65536 | tf_op jit(solution)/shard_map/psum | solution.py:31
  239.4 2.0 select_convert_fusion.3
  241.4 16.6 %all_gather.20 = bf16[8,16384]{1,0:T(8,128)(2,1)S(1)} all-gather(bf16[8,1024]{1,0:T(8,128)(2,1)S(1)} %get-tuple-element.17), channel_id=1, replica_groups=mesh['row'=16,'col'=32] {'row'}, dimensions={1}, use_global_device_ids=true | all-gather | bytes 278528 | tf_op jit(solution)/shard_map/all_gather | solution.py:42
  258.4 94.9 %psum.51 = f32[8,1024]{1,0:T(8,128)S(1)} all-reduce(f32[8,1024]{1,0:T(8,128)S(1)} %convolution_add_fusion), channel_id=1, replica_groups=mesh['row'=16,'col'=32] {'col'}, use_global_device_ids=true, to_apply=%region_3.4 | all-reduce | flops 8192 | bytes 65536 | tf_op jit(solution)/shard_map/psum | solution.py:31
  353.3 2.0 bitcast_select_fusion.5
  355.3 1.6 fusion.22
  357.1 58.2 %psum.52 = f32[8,512]{1,0:T(8,128)S(1)} all-reduce(f32[8,512]{1,0:T(8,128)S(1)} %fusion.40), channel_id=1, replica_groups=mesh['row'=16,'col'=32] {'row'}, use_global_device_ids=true, to_apply=%region_4.5 | all-reduce | flops 4096 | bytes 32768 | tf_op jit(solution)/shard_map/psum | solution.py:49
  415.3 45.4 %all_gather.21 = f32[8,16384]{1,0:T(8,128)S(1)} all-gather(f32[8,512]{1,0:T(8,128)S(1)} %psum.52), channel_id=1, replica_groups=mesh['row'=16,'col'=32] {'col'}, dimensions={1}, use_global_device_ids=true | all-gather | bytes 540672 | tf_op jit(solution)/shard_map/all_gather | solution.py:50
  460.8 1.6 bitcast_select_fusion.3
  462.6 55.9 %psum.53 = f32[8,512]{1,0:T(8,128)S(1)} all-reduce(f32[8,512]{1,0:T(8,128)S(1)} %convolution_add_fusion.3), channel_id=1, replica_groups=mesh['row'=16,'col'=32] {'row'}, use_global_device_ids=true, to_apply=%region_5.6 | all-reduce | flops 4096 | bytes 32768 | tf_op jit(solution)/shard_map/psum | solution.py:49
  518.5 44.6 %all_gather.22 = f32[8,16384]{1,0:T(8,128)S(1)} all-gather(f32[8,512]{1,0:T(8,128)S(1)} %psum.53), channel_id=1, replica_groups=mesh['row'=16,'col'=32] {'col'}, dimensions={1}, use_global_device_ids=true | all-gather | bytes 540672 | tf_op jit(solution)/shard_map/all_gather | solution.py:50
  563.1 1.6 fusion.18
  564.9 55.8 %psum.54 = f32[8,512]{1,0:T(8,128)S(1)} all-reduce(f32[8,512]{1,0:T(8,128)S(1)} %convolution_add_fusion.2), channel_id=1, replica_groups=mesh['row'=16,'col'=32] {'row'}, use_global_device_ids=true, to_apply=%region_6.7 | all-reduce | flops 4096 | bytes 32768 | tf_op jit(solution)/shard_map/psum | solution.py:49
  620.6 42.0 %all_gather.23 = f32[8,16384]{1,0:T(8,128)S(1)} all-gather(f32[8,512]{1,0:T(8,128)S(1)} %psum.54), channel_id=1, replica_groups=mesh['row'=16,'col'=32] {'col'}, dimensions={1}, use_global_device_ids=true | all-gather | bytes 540672 | tf_op jit(solution)/shard_map/all_gather | solution.py:50
  662.6 1.6 bitcast_select_fusion.1
  664.8 99.5 %psum.55 = bf16[8,1024]{1,0:T(8,128)(2,1)S(1)} all-reduce(f32[8,1024]{1,0:T(8,128)S(1)} %fusion.2), channel_id=1, replica_groups=mesh['row'=16,'col'=32] {'row','col'}, use_global_device_ids=true, to_apply=%region_7.8 | all-reduce | flops 8192 | bytes 49152 | tf_op jit(solution)/shard_map/psum | solution.py:69
  764.8 0.7 copy.11
  (22 shorter events, 2.6 us)
Async XLA Ops:
  0.6 663.6 %copy-start = (bf16[1024,1,1024]{2,0,1:T(8,128)(2,1)S(1)}, bf16[1024,1,1024]{2,0,1:T(8,128)(2,1)}, u32[]{:S(2)}) copy-start(bf16[1024,1,1024]{2,0,1:T(8,128)(2,1)} %param.13) | copy-start | bytes 6291460
  0.6 143.2 %copy-start.1 = (bf16[1024,512]{1,0:T(8,128)(2,1)S(1)}, bf16[1024,512]{1,0:T(8,128)(2,1)}, u32[]{:S(2)}) copy-start(bf16[1024,512]{1,0:T(8,128)(2,1)} %param.7) | copy-start | bytes 3145732
  0.7 123.3 %copy-start.2 = (f32[8,1024]{1,0:T(8,128)S(1)}, f32[8,1024]{1,0:T(8,128)}, u32[]{:S(2)}) copy-start(f32[8,1024]{1,0:T(8,128)} %param.9) | copy-start | bytes 98308
  462.6 201.6 %copy-start.4 = (f32[1,1024]{1,0:T(1,128)S(1)}, f32[1,1024]{1,0:T(1,128)}, u32[]{:S(2)}) copy-start(f32[1,1024]{1,0:T(1,128)} %param.11) | copy-start | bytes 12292
  462.6 201.6 %copy-start.5 = (f32[1,1024]{1,0:T(1,128)S(1)}, f32[1,1024]{1,0:T(1,128)}, u32[]{:S(2)}) copy-start(f32[1,1024]{1,0:T(1,128)} %param.12) | copy-start | bytes 12292
  664.2 100.6 %copy-start.3 = (f32[8,1024]{1,0:T(8,128)}, f32[8,1024]{1,0:T(8,128)S(1)}, u32[]{:S(2)}) copy-start(f32[8,1024]{1,0:T(8,128)S(1)} %get-tuple-element.23) | copy-start | bytes 98308
where the time goes:
time: 766 us; the launch traced here: 765 us
  blocking collectives  745 us (97%)
  matrix products  18.2 us (2%)
    psum x3, blocking collectives, on_device(): total_sum = lax.psum(pending, 'col')  289 us
    psum x3, blocking collectives, on_device(): column_sum = lax.psum(back_pending, 'row')  170 us
    all_gather x3, blocking collectives, on_device(): full_sum = lax.all_gather(column_sum, 'col', axis=1, tiled=True)  132 us
    psum x1, blocking collectives, on_device(): coords = lax.psum(partial_coords, ('row', 'col'))  99.5 us
    all_gather x3, blocking collectives, on_device(): whole = lax.all_gather(fresh, 'row', axis=1, tiled=True)  54.2 us

commit v1 on v0

v1 whole, which is shorter than its diff:
```python
import jax
import jax.numpy as jnp
from jax import lax
from jax.sharding import Mesh, PartitionSpec as P

LEVELS = 4
PLANE = ("x", "y")

highest = lax.Precision.HIGHEST


def spread(value, axes, count):
    return lax.all_to_all(jnp.broadcast_to(value[None], (count,) + value.shape), axes, 0, 0, tiled=True)


def both_cores(value):
    return lax.all_gather(value, "k", axis=0)


def on_device(front, diag_inverse, load, panel_order, tie, mass, modes):
    vectors = load.shape[0]
    block_size = diag_inverse.shape[1]
    local_panels = diag_inverse.shape[0]
    rows_local = front.shape[0]
    half = front.shape[1]
    half_panels = half // block_size
    panels = panel_order.shape[0]
    plane_at = lax.axis_index(PLANE)
    z_at = lax.axis_index("z")
    core_at = lax.axis_index("k")
    plane_size = lax.axis_size(PLANE)
    z_size = lax.axis_size("z")

    first_panel = plane_at * local_panels + core_at * half_panels
    mine_ids = first_panel + jnp.arange(half_panels, dtype=jnp.int32)
    counting = jnp.arange(panels, dtype=jnp.int32)
    ranks = jnp.sum(jnp.where(panel_order[None, :] == mine_ids[:, None], counting[None, :], 0), axis=1)
    level_of = jnp.repeat(ranks // (panels // LEVELS), block_size)[None, :]

    inverse = lax.dynamic_slice_in_dim(diag_inverse, core_at * half_panels, half_panels, 0)
    load_half = lax.dynamic_slice_in_dim(load, core_at * half, half, 1)

    def solve(value, form):
        value = value.reshape(vectors, half_panels, block_size)
        return jnp.einsum(form, value, inverse, precision=highest).reshape(vectors, half)

    def my_half_sum(value):
        pair = both_cores(value)
        total = pair[0] + pair[1]
        return jnp.where(core_at == 0, total[:, :half], total[:, half:])

    def join(value):
        pair = both_cores(value)
        return jnp.concatenate([pair[0], pair[1]], axis=1)

    def total_over(value, axes, count):
        return jnp.sum(spread(value.astype(jnp.bfloat16), axes, count).astype(jnp.float32), axis=0)

    pending = jnp.zeros((vectors, rows_local), jnp.float32)
    forward_out = jnp.zeros((vectors, half), jnp.float32)
    for level in range(LEVELS):
        remain = load_half
        if level > 0:
            remain = load_half - total_over(my_half_sum(pending), "z", z_size)
        chosen = level_of == level
        candidate = solve(remain, "vpj,pij->vpi")
        forward_out = jnp.where(chosen, candidate, forward_out)
        if level < LEVELS - 1:
            fresh = jnp.where(chosen, candidate, 0.0).astype(jnp.bfloat16)
            mine = lax.dynamic_index_in_dim(spread(fresh, PLANE, plane_size), z_at, 0, keepdims=False)
            pending = pending + lax.dot_general(
                mine, front, (((1,), (1,)), ((), ())), preferred_element_type=jnp.float32
            )

    back_pending = jnp.zeros((vectors, half), jnp.float32)
    back_out = jnp.zeros((vectors, half), jnp.float32)
    for level in reversed(range(LEVELS)):
        chosen = level_of == level
        if level == LEVELS - 1:
            solved = jnp.where(chosen, solve(forward_out, "vpj,pji->vpi"), 0.0)
            back_out = solved
            fresh = solved.astype(jnp.bfloat16)
        else:
            here = total_over(back_pending, PLANE, plane_size)
            solved = jnp.where(chosen, solve(forward_out - here, "vpj,pji->vpi"), 0.0).astype(jnp.bfloat16)
            fresh = lax.dynamic_index_in_dim(spread(solved, "z", z_size), plane_at, 0, keepdims=False)
            back_out = back_out + fresh.astype(jnp.float32)
        if level > 0:
            back_pending = back_pending + jnp.dot(join(fresh), front, preferred_element_type=jnp.float32)

    solution_rows = join(back_out)
    static = tie * solution_rows
    weighted = (mass * static).astype(jnp.bfloat16)
    mode_rows = modes.reshape(modes.shape[0], -1)
    coords = lax.dot_general(
        weighted, mode_rows, (((1,), (1,)), ((), ())), preferred_element_type=jnp.float32
    )
    coords = total_over(my_half_sum(coords), PLANE, plane_size)
    coords = total_over(coords, "z", z_size)
    coords = join(coords.astype(jnp.bfloat16))
    correction = jnp.dot(coords, mode_rows, preferred_element_type=jnp.float32)
    return solution_rows, (static - correction)[:, None, :]


def solution(mesh):
    grid = Mesh(mesh.devices.reshape(4, 4, 16, 2), ("x", "y", "z", "k"))
    row, col = PLANE, ("z", "k")
    in_specs = (
        P(row, col),
        P(row, None, None),
        P(None, row),
        P(),
        P(col, row),
        P(col, row),
        P(None, col, row),
    )
    out_specs = (P(None, row), P(None, col, row))
    return jax.shard_map(
        on_device, mesh=grid, in_specs=in_specs, out_specs=out_specs, check_vma=False
    )
```

time: 766 us -> 259 us (0.34)
  blocking collectives: 745 us -> 151 us
  waiting for transfers between devices: 0 us -> 54.7 us
  starting transfers between devices: 0 us -> 32.2 us
    psum x7 -> x0, blocking collectives: 559 us -> none  [the longest x3 289 us: on_device(): total_sum = lax.psum(pending, 'col')]
    all_gather x6 -> x9, blocking collectives: 186 us -> 46.4 us  [both_cores(): return lax.all_gather(value, 'k', axis=0)]
    all_to_all x0 -> x9, blocking collectives: none -> 105 us  [spread(): lax.all_to_all(jnp.broadcast_to(value[None], (count,) + value.shape), axe...]
    all_to_all x0 -> x5, waiting for transfers between devices: none -> 54.7 us  [spread(): lax.all_to_all(jnp.broadcast_to(value[None], (count,) + value.shape), axe...]
    all_to_all x0 -> x5, starting transfers between devices: none -> 32.2 us  [spread(): lax.all_to_all(jnp.broadcast_to(value[None], (count,) + value.shape), axe...]
  transfers between devices with their start and end apart: 0 -> 5, of which waited for: 0 -> 5; matrix products, arithmetic and copies ran while one was open for 0% -> 0% of each run, Pallas kernels for 0% -> 0%
where the time goes in v1:
time: 259 us; the launch traced here: 258 us
  blocking collectives  151 us (58%)
  waiting for transfers between devices  54.7 us (21%)
  starting transfers between devices  32.2 us (12%)
  matrix products  13.3 us (5%)
  local copies, waits for them, and re-layouts  4.5 us (2%)
    all_to_all x9, blocking collectives, spread(): lax.all_to_all(jnp.broadcast_to(value[None], (count,) + value.shape), axe...  105 us
    all_to_all x5, waiting for transfers between devices, spread(): lax.all_to_all(jnp.broadcast_to(value[None], (count,) + value.shape), axe...  54.7 us
    all_gather x9, blocking collectives, both_cores(): return lax.all_gather(value, 'k', axis=0)  46.4 us
    all_to_all x5, starting transfers between devices, spread(): lax.all_to_all(jnp.broadcast_to(value[None], (count,) + value.shape), axe...  32.2 us
    dot_general x8, matrix products, solve(): jnp.einsum(form, value, inverse, precision=highest).reshape(vectors, half)  9.22 us
  transfers between devices with their start and end apart: 5, of which 5 were waited for; matrix products, arithmetic and copies ran while one was open for 0% of the time, Pallas kernels for 0%

profile of v1, /device:TPU:1, one launch (start us, length us, event | category | flops | bytes accessed | tf_op | source)
XLA Modules:
  0.0 258.2 jit_solution(1437403199508348338)
XLA Ops:
  3.9 7.6 %all-to-all-start = ((bf16[16,8,512]{2,1,0:T(8,128)(2,1)}), bf16[16,8,512]{2,1,0:T(8,128)(2,1)S(1)}, u32[]{:S(2)}, u32[]{:S(2)}) async-start(bf16[16,8,512]{2,1,0:T(8,128)(2,1)} %broadcast_in_dim.189), calls=%async_computation | async-start | bytes 262144 | tf_op jit(solution)/shard_map/all_to_all | solution.py:13
  11.5 6.7 %all-to-all-done = bf16[16,8,512]{2,1,0:T(8,128)(2,1)S(1)} async-done(((bf16[16,8,512]{2,1,0:T(8,128)(2,1)}), bf16[16,8,512]{2,1,0:T(8,128)(2,1)S(1)}, u32[]{:S(2)}, u32[]{:S(2)}) %all-to-all-start) | async-done | bytes 131104 | tf_op jit(solution)/shard_map/all_to_all | solution.py:13
  19.8 5.4 %all-gather = f32[16,1024]{1,0:T(8,128)S(1)} all-gather(f32[8,1024]{1,0:T(8,128)S(1)} %fusion.65), channel_id=2, replica_groups=mesh['x'=4,'y'=4,'z'=16,'k'=2] {'k'}, dimensions={0}, use_global_device_ids=true | all-gather | bytes 98304 | tf_op jit(solution)/shard_map/all_gather | solution.py:17
  25.8 13.2 %all-to-all-start.1 = ((bf16[16,8,512]{2,1,0:T(8,128)(2,1)}), bf16[16,8,512]{2,1,0:T(8,128)(2,1)S(1)}, u32[]{:S(2)}, u32[]{:S(2)}) async-start(bf16[16,8,512]{2,1,0:T(8,128)(2,1)} %broadcast_in_dim.192), calls=%async_computation.1 | async-start | bytes 262144 | tf_op jit(solution)/shard_map/all_to_all | solution.py:13
  39.1 12.0 %all-to-all-done.1 = bf16[16,8,512]{2,1,0:T(8,128)(2,1)S(1)} async-done(((bf16[16,8,512]{2,1,0:T(8,128)(2,1)}), bf16[16,8,512]{2,1,0:T(8,128)(2,1)S(1)}, u32[]{:S(2)}, u32[]{:S(2)}) %all-to-all-start.1) | async-done | bytes 131104 | tf_op jit(solution)/shard_map/all_to_all | solution.py:13
  52.6 9.8 %all_to_all.70 = bf16[16,8,512]{2,1,0:T(8,128)(2,1)S(1)} all-to-all(bf16[16,8,512]{2,1,0:T(8,128)(2,1)S(1)} %broadcast_in_dim.193), channel_id=1, replica_groups=mesh['x'=4,'y'=4,'z'=16,'k'=2] {'x','y'}, dimensions={0} | all-to-all | bytes 262144 | tf_op jit(solution)/shard_map/all_to_all | solution.py:13
  62.8 6.2 %all-gather.1 = f32[16,1024]{1,0:T(8,128)S(1)} all-gather(f32[8,1024]{1,0:T(8,128)S(1)} %convolution_add_fusion.1), channel_id=3, replica_groups=mesh['x'=4,'y'=4,'z'=16,'k'=2] {'k'}, dimensions={0}, use_global_device_ids=true | all-gather | bytes 98304 | tf_op jit(solution)/shard_map/all_gather | solution.py:17
  73.6 12.0 %all-to-all-done.3 = bf16[16,8,512]{2,1,0:T(8,128)(2,1)S(1)} async-done(((bf16[16,8,512]{2,1,0:T(8,128)(2,1)}), bf16[16,8,512]{2,1,0:T(8,128)(2,1)S(1)}, u32[]{:S(2)}, u32[]{:S(2)}) %all-to-all-start.3) | async-done | bytes 131104 | tf_op jit(solution)/shard_map/all_to_all | solution.py:13
  87.2 9.8 %all_to_all.71 = bf16[16,8,512]{2,1,0:T(8,128)(2,1)S(1)} all-to-all(bf16[16,8,512]{2,1,0:T(8,128)(2,1)S(1)} %broadcast_in_dim.197), channel_id=1, replica_groups=mesh['x'=4,'y'=4,'z'=16,'k'=2] {'x','y'}, dimensions={0} | all-to-all | bytes 262144 | tf_op jit(solution)/shard_map/all_to_all | solution.py:13
  97.4 6.2 %all-gather.2 = f32[16,1024]{1,0:T(8,128)S(1)} all-gather(f32[8,1024]{1,0:T(8,128)S(1)} %convolution_add_fusion), channel_id=4, replica_groups=mesh['x'=4,'y'=4,'z'=16,'k'=2] {'k'}, dimensions={0}, use_global_device_ids=true | all-gather | bytes 98304 | tf_op jit(solution)/shard_map/all_gather | solution.py:17
  108.2 12.0 %all-to-all-done.5 = bf16[16,8,512]{2,1,0:T(8,128)(2,1)S(1)} async-done(((bf16[16,8,512]{2,1,0:T(8,128)(2,1)}), bf16[16,8,512]{2,1,0:T(8,128)(2,1)S(1)}, u32[]{:S(2)}, u32[]{:S(2)}) %all-to-all-start.5) | async-done | bytes 131104 | tf_op jit(solution)/shard_map/all_to_all | solution.py:13
  123.1 4.8 %all_gather.52 = bf16[2,8,512]{2,1,0:T(8,128)(2,1)S(1)} all-gather(bf16[1,8,512]{2,1,0:T(8,128)(2,1)S(1)} %get-tuple-element.29), channel_id=1, replica_groups=mesh['x'=4,'y'=4,'z'=16,'k'=2] {'k'}, dimensions={0}, use_global_device_ids=true | all-gather | bytes 24576 | tf_op jit(solution)/shard_map/all_gather | solution.py:17
  128.1 9.8 %all_to_all.72 = bf16[16,8,512]{2,1,0:T(8,128)(2,1)S(1)} all-to-all(bf16[16,8,512]{2,1,0:T(8,128)(2,1)S(1)} %broadcast_in_dim.204), channel_id=1, replica_groups=mesh['x'=4,'y'=4,'z'=16,'k'=2] {'x','y'}, dimensions={0} | all-to-all | bytes 262144 | tf_op jit(solution)/shard_map/all_to_all | solution.py:13
  142.8 12.0 %all-to-all-done.7 = bf16[16,8,512]{2,1,0:T(8,128)(2,1)S(1)} async-done(((bf16[16,8,512]{2,1,0:T(8,128)(2,1)}), bf16[16,8,512]{2,1,0:T(8,128)(2,1)S(1)}, u32[]{:S(2)}, u32[]{:S(2)}) %all-to-all-start.7) | async-done | bytes 131104 | tf_op jit(solution)/shard_map/all_to_all | solution.py:13
  154.7 5.6 %all_gather.53 = bf16[2,8,512]{2,1,0:T(8,128)(2,1)S(1)} all-gather(bf16[1,8,512]{2,1,0:T(8,128)(2,1)S(1)} %constant_dynamic-slice_fusion.1), channel_id=1, replica_groups=mesh['x'=4,'y'=4,'z'=16,'k'=2] {'k'}, dimensions={0}, use_global_device_ids=true | all-gather | bytes 24576 | tf_op jit(solution)/shard_map/all_gather | solution.py:17
  160.6 10.0 %all_to_all.73 = bf16[16,8,512]{2,1,0:T(8,128)(2,1)S(1)} all-to-all(bf16[16,8,512]{2,1,0:T(8,128)(2,1)S(1)} %broadcast_in_dim.206), channel_id=1, replica_groups=mesh['x'=4,'y'=4,'z'=16,'k'=2] {'x','y'}, dimensions={0} | all-to-all | bytes 262144 | tf_op jit(solution)/shard_map/all_to_all | solution.py:13
  171.9 15.2 %all_to_all.74 = bf16[16,8,512]{2,1,0:T(8,128)(2,1)S(1)} all-to-all(bf16[16,8,512]{2,1,0:T(8,128)(2,1)S(1)} %broadcast_in_dim.207), channel_id=1, replica_groups=mesh['x'=4,'y'=4,'z'=16,'k'=2] {'z'}, dimensions={0} | all-to-all | bytes 262144 | tf_op jit(solution)/shard_map/all_to_all | solution.py:13
  187.2 5.5 %all_gather.54 = bf16[2,8,512]{2,1,0:T(8,128)(2,1)S(1)} all-gather(bf16[1,8,512]{2,1,0:T(8,128)(2,1)S(1)} %constant_dynamic-slice_fusion), channel_id=1, replica_groups=mesh['x'=4,'y'=4,'z'=16,'k'=2] {'k'}, dimensions={0}, use_global_device_ids=true | all-gather | bytes 24576 | tf_op jit(solution)/shard_map/all_gather | solution.py:17
  192.9 9.9 %all_to_all.75 = bf16[16,8,512]{2,1,0:T(8,128)(2,1)S(1)} all-to-all(bf16[16,8,512]{2,1,0:T(8,128)(2,1)S(1)} %broadcast_in_dim.208), channel_id=1, replica_groups=mesh['x'=4,'y'=4,'z'=16,'k'=2] {'x','y'}, dimensions={0} | all-to-all | bytes 262144 | tf_op jit(solution)/shard_map/all_to_all | solution.py:13
  203.2 15.2 %all_to_all.76 = bf16[16,8,512]{2,1,0:T(8,128)(2,1)S(1)} all-to-all(bf16[16,8,512]{2,1,0:T(8,128)(2,1)S(1)} %broadcast_in_dim.209), channel_id=1, replica_groups=mesh['x'=4,'y'=4,'z'=16,'k'=2] {'z'}, dimensions={0} | all-to-all | bytes 262144 | tf_op jit(solution)/shard_map/all_to_all | solution.py:13
  218.4 5.5 %all_gather.55 = f32[2,8,512]{2,1,0:T(8,128)S(1)} all-gather(f32[1,8,512]{2,1,0:T(8,128)S(1)} %convert_add_fusion), channel_id=1, replica_groups=mesh['x'=4,'y'=4,'z'=16,'k'=2] {'k'}, dimensions={0}, use_global_device_ids=true | all-gather | bytes 49152 | tf_op jit(solution)/shard_map/all_gather | solution.py:17
  226.5 9.9 %all_to_all.77 = bf16[16,8,512]{2,1,0:T(8,128)(2,1)S(1)} all-to-all(bf16[16,8,512]{2,1,0:T(8,128)(2,1)S(1)} %broadcast_in_dim.210), channel_id=1, replica_groups=mesh['x'=4,'y'=4,'z'=16,'k'=2] {'x','y'}, dimensions={0} | all-to-all | bytes 262144 | tf_op jit(solution)/shard_map/all_to_all | solution.py:13
  236.4 15.2 %all_to_all.78 = bf16[16,8,512]{2,1,0:T(8,128)(2,1)S(1)} all-to-all(bf16[16,8,512]{2,1,0:T(8,128)(2,1)S(1)} %broadcast_in_dim.211), channel_id=1, replica_groups=mesh['x'=4,'y'=4,'z'=16,'k'=2] {'z'}, dimensions={0} | all-to-all | bytes 262144 | tf_op jit(solution)/shard_map/all_to_all | solution.py:13
  251.7 5.5 %all-gather.4 = bf16[16,512]{1,0:T(8,128)(2,1)S(1)} all-gather(bf16[8,512]{1,0:T(8,128)(2,1)S(1)} %reduce_sum.104), channel_id=6, replica_groups=mesh['x'=4,'y'=4,'z'=16,'k'=2] {'k'}, dimensions={0}, use_global_device_ids=true | all-gather | bytes 24576 | tf_op jit(solution)/shard_map/all_gather | solution.py:17
  (84 shorter events, 32.4 us)
Async XLA Ops:
  0.6 223.3 %copy-start = (bf16[1024,1,1024]{2,0,1:T(8,128)(2,1)S(1)}, bf16[1024,1,1024]{2,0,1:T(8,128)(2,1)}, u32[]{:S(2)}) copy-start(bf16[1024,1,1024]{2,0,1:T(8,128)(2,1)} %param.13) | copy-start | bytes 6291460
  0.6 50.5 %copy-start.5 = (f32[8,1024]{1,0:T(8,128)S(1)}, f32[8,1024]{1,0:T(8,128)}, u32[]{:S(2)}) copy-start(f32[8,1024]{1,0:T(8,128)} %param.9) | copy-start | bytes 98308
  0.7 61.8 %copy-start.1 = (bf16[1024,512]{1,0:T(8,128)(2,1)S(1)}, bf16[1024,512]{1,0:T(8,128)(2,1)}, u32[]{:S(2)}) copy-start(bf16[1024,512]{1,0:T(8,128)(2,1)} %param.7) | copy-start | bytes 3145732
  3.9 14.3 %all-to-all-start = ((bf16[16,8,512]{2,1,0:T(8,128)(2,1)}), bf16[16,8,512]{2,1,0:T(8,128)(2,1)S(1)}, u32[]{:S(2)}, u32[]{:S(2)}) async-start(bf16[16,8,512]{2,1,0:T(8,128)(2,1)} %broadcast_in_dim.189), calls=%async_computation | async-start | bytes 262144 | tf_op jit(solution)/shard_map/all_to_all | solution.py:13
  25.8 25.3 %all-to-all-start.1 = ((bf16[16,8,512]{2,1,0:T(8,128)(2,1)}), bf16[16,8,512]{2,1,0:T(8,128)(2,1)S(1)}, u32[]{:S(2)}, u32[]{:S(2)}) async-start(bf16[16,8,512]{2,1,0:T(8,128)(2,1)} %broadcast_in_dim.192), calls=%async_computation.1 | async-start | bytes 262144 | tf_op jit(solution)/shard_map/all_to_all | solution.py:13
  69.7 15.9 %all-to-all-start.3 = ((bf16[16,8,512]{2,1,0:T(8,128)(2,1)}), bf16[16,8,512]{2,1,0:T(8,128)(2,1)S(1)}, u32[]{:S(2)}, u32[]{:S(2)}) async-start(bf16[16,8,512]{2,1,0:T(8,128)(2,1)} %broadcast_in_dim.196), calls=%async_computation.3 | async-start | bytes 262144 | tf_op jit(solution)/shard_map/all_to_all | solution.py:13
  104.3 15.9 %all-to-all-start.5 = ((bf16[16,8,512]{2,1,0:T(8,128)(2,1)}), bf16[16,8,512]{2,1,0:T(8,128)(2,1)S(1)}, u32[]{:S(2)}, u32[]{:S(2)}) async-start(bf16[16,8,512]{2,1,0:T(8,128)(2,1)} %broadcast_in_dim.198), calls=%async_computation.5 | async-start | bytes 262144 | tf_op jit(solution)/shard_map/all_to_all | solution.py:13
  120.2 17.7 %copy-start.2 = (f32[8,128,128]{2,1,0:T(8,128)S(1)}, f32[8,128,128]{2,1,0:T(8,128)}, u32[]{:S(2)}) copy-start(f32[8,128,128]{2,1,0:T(8,128)} %param.8) | copy-start | bytes 1572868
  138.9 15.8 %all-to-all-start.7 = ((bf16[16,8,512]{2,1,0:T(8,128)(2,1)}), bf16[16,8,512]{2,1,0:T(8,128)(2,1)S(1)}, u32[]{:S(2)}, u32[]{:S(2)}) async-start(bf16[16,8,512]{2,1,0:T(8,128)(2,1)} %broadcast_in_dim.205), calls=%async_computation.7 | async-start | bytes 262144 | tf_op jit(solution)/shard_map/all_to_all | solution.py:13
  154.7 48.1 %copy-start.3 = (f32[8,128,128]{2,1,0:T(8,128)S(1)}, f32[8,128,128]{2,1,0:T(8,128)}, u32[]{:S(2)}) copy-start(f32[8,128,128]{2,1,0:T(8,128)} %param.8) | copy-start | bytes 1572868
  160.6 63.4 %copy-start.6 = (f32[1,1024]{1,0:T(1,128)S(1)}, f32[1,1024]{1,0:T(1,128)}, u32[]{:S(2)}) copy-start(f32[1,1024]{1,0:T(1,128)} %param.11) | copy-start | bytes 12292
  160.6 63.4 %copy-start.7 = (f32[1,1024]{1,0:T(1,128)S(1)}, f32[1,1024]{1,0:T(1,128)}, u32[]{:S(2)}) copy-start(f32[1,1024]{1,0:T(1,128)} %param.12) | copy-start | bytes 12292
  223.9 33.6 %copy-start.4 = (f32[8,1024]{1,0:T(8,128)}, f32[8,1024]{1,0:T(8,128)S(1)}, u32[]{:S(2)}) copy-start(f32[8,1024]{1,0:T(8,128)S(1)} %pad_maximum_fusion) | copy-start | bytes 98308

commit v2 on v1

v2 whole, which is shorter than its diff:
```python
import jax
import jax.numpy as jnp
from jax import lax
from jax.experimental import pallas as pl
from jax.experimental.pallas import tpu as pltpu
from jax.sharding import Mesh, PartitionSpec as P

LEVELS = 4
PLANE = ("x", "y")
F32, BF16 = jnp.float32, jnp.bfloat16


def matmul(a, b, form):
    dims = {"nn": (((1,), (0,)), ((), ())), "nt": (((1,), (1,)), ((), ()))}[form]
    return lax.dot_general(a, b, dims, preferred_element_type=F32)


def split(value):
    high = value.astype(BF16)
    return high, (value - high.astype(F32)).astype(BF16)


class Far:
    def __init__(self, array):
        self.array = array


def call(body, outs, *args, scratch=()):
    vmem = pl.BlockSpec(memory_space=pltpu.VMEM)
    in_specs, given = [], []
    for arg in args:
        if isinstance(arg, Far):
            in_specs.append(pl.BlockSpec(memory_space=pltpu.HBM))
            given.append(pltpu.with_memory_space_constraint(arg.array, pltpu.HBM))
        else:
            in_specs.append(vmem)
            given.append(pltpu.with_memory_space_constraint(arg, pltpu.VMEM))
    return pl.pallas_call(
        body,
        out_shape=[out if isinstance(out, jax.ShapeDtypeStruct) else pltpu.VMEM(*out) for out in outs],
        in_specs=in_specs,
        out_specs=[vmem] * len(outs),
        scratch_shapes=list(scratch),
        compiler_params=pltpu.CompilerParams(vmem_limit_bytes=8 << 20),
    )(*given)


def send_to_all(out_ref, value):
    value = value.astype(BF16)
    for slot in range(out_ref.shape[0]):
        out_ref[slot] = value


def sum_slots(ref):
    total = ref[0].astype(F32)
    for slot in range(1, ref.shape[0]):
        total = total + ref[slot].astype(F32)
    return total


def solve(value, high_ref, low_ref, form):
    panels, block = high_ref.shape[0], high_ref.shape[1]
    out = []
    for p in range(panels):
        top, rest = split(value[:, p * block : (p + 1) * block])
        out.append(
            matmul(top, high_ref[p], form) + (matmul(rest, high_ref[p], form) + matmul(top, low_ref[p], form))
        )
    return jnp.concatenate(out, axis=1)


def start_kernel(
    order_hbm, load_hbm, inverse_hbm, front_hbm,
    level_ref, high_ref, low_ref, mine_ref, y_ref, send_ref, front_ref,
    order_ref, inverse_ref, sems,
):
    panels, block = high_ref.shape[0], high_ref.shape[1]
    half = panels * block
    core = lax.axis_index("k")
    copies = [
        pltpu.make_async_copy(order_hbm, order_ref, sems.at[0]),
        pltpu.make_async_copy(inverse_hbm.at[pl.ds(core * panels, panels)], inverse_ref, sems.at[1]),
        pltpu.make_async_copy(load_hbm.at[:, pl.ds(pl.multiple_of(core * half, half), half)], mine_ref, sems.at[2]),
        pltpu.make_async_copy(front_hbm, front_ref, sems.at[3]),
    ]
    for copy in copies:
        copy.start()
    copies[0].wait()
    order = order_ref[...]
    counting = lax.broadcasted_iota(jnp.int32, order.shape, 1)
    per_level = order.shape[1] // LEVELS
    first = lax.axis_index(PLANE) * (2 * panels) + core * panels
    levels = []
    for p in range(panels):
        rank = jnp.sum(jnp.where(order == first + p, counting, 0), axis=1, keepdims=True)
        level = jnp.zeros_like(rank)
        for bound in range(1, LEVELS):
            level = level + jnp.where(rank >= bound * per_level, 1, 0)
        levels.append(jnp.broadcast_to(level, (level_ref.shape[0], block)))
    level_row = jnp.concatenate(levels, axis=1)
    level_ref[...] = level_row
    copies[1].wait()
    high, low = split(inverse_ref[...])
    high_ref[...] = high
    low_ref[...] = low
    copies[2].wait()
    y = jnp.where(level_row == 0, solve(mine_ref[...], high_ref, low_ref, "nt"), 0.0)
    y_ref[...] = y
    send_to_all(send_ref, y)
    copies[3].wait()


def update_kernel(front_ref, got_ref, *refs):
    out_ref = refs[-1]
    out = matmul(got_ref[lax.axis_index("z")], front_ref[...], "nt")
    if len(refs) == 2:
        out = refs[0][...] + out
    out_ref[...] = out


def pair_kernel(pair_ref, send_ref):
    half = send_ref.shape[2]
    rows = pair_ref[0] + pair_ref[1]
    send_to_all(send_ref, jnp.where(lax.axis_index("k") == 0, rows[:, :half], rows[:, half:]))


def forward_kernel(level, got_ref, mine_ref, level_ref, high_ref, low_ref, y_in_ref, y_ref, send_ref):
    chosen = level_ref[...] == level
    candidate = solve(mine_ref[...] - sum_slots(got_ref), high_ref, low_ref, "nt")
    y_ref[...] = jnp.where(chosen, candidate, y_in_ref[...])
    send_to_all(send_ref, jnp.where(chosen, candidate, 0.0))


def turn_kernel(
    got_ref, mine_ref, level_ref, high_ref, low_ref, y_in_ref, modes_hbm, y_ref, x_ref, fresh_ref, modes_ref, sem
):
    modes_copy = pltpu.make_async_copy(modes_hbm, modes_ref, sem)
    modes_copy.start()
    chosen = level_ref[...] == LEVELS - 1
    candidate = solve(mine_ref[...] - sum_slots(got_ref), high_ref, low_ref, "nt")
    y = jnp.where(chosen, candidate, y_in_ref[...])
    y_ref[...] = y
    x = jnp.where(chosen, solve(y, high_ref, low_ref, "nn"), 0.0)
    x_ref[...] = x
    fresh_ref[...] = x.astype(BF16)
    modes_copy.wait()


def back_update_kernel(first, last, front_ref, pair_ref, *refs):
    half = pair_ref.shape[2]
    out = matmul(pair_ref[0], front_ref[:half], "nn") + matmul(pair_ref[1], front_ref[half:], "nn")
    if not first:
        out = refs[0][...] + out
    if not last:
        refs[-2][...] = out
    send_to_all(refs[-1], out)


def back_kernel(level, got_ref, level_ref, high_ref, low_ref, y_ref, send_ref):
    x = solve(y_ref[...] - sum_slots(got_ref), high_ref, low_ref, "nn")
    send_to_all(send_ref, jnp.where(level_ref[...] == level, x, 0.0))


def pick_kernel(got_ref, x_in_ref, x_ref, fresh_ref):
    fresh = got_ref[lax.axis_index(PLANE)]
    x_ref[...] = x_in_ref[...] + fresh.astype(F32)
    fresh_ref[...] = fresh


def last_pick_kernel(got_ref, x_in_ref, x_ref):
    x_ref[...] = x_in_ref[...] + got_ref[lax.axis_index(PLANE)].astype(F32)


def coords_kernel(pair_ref, tie_ref, mass_ref, modes_ref, x_ref, static_ref, send_ref):
    x = jnp.concatenate([pair_ref[0], pair_ref[1]], axis=1)
    x_ref[...] = x
    static = tie_ref[...] * x
    static_ref[...] = static
    coords = matmul((mass_ref[...] * static).astype(BF16), modes_ref[...], "nt").astype(BF16)
    cores, half = 2, send_ref.shape[2]
    for slot in range(send_ref.shape[0]):
        part = slot % cores
        send_ref[slot] = coords[:, part * half : (part + 1) * half]


def relay_kernel(got_ref, send_ref):
    send_to_all(send_ref, sum_slots(got_ref))


def gathered_kernel(got_ref, out_ref):
    out_ref[...] = sum_slots(got_ref).astype(BF16)


def finish_kernel(static_ref, pair_ref, modes_ref, x_ref, whole_ref, out_ref):
    half = pair_ref.shape[2]
    correction = matmul(pair_ref[0], modes_ref[:half], "nn") + matmul(pair_ref[1], modes_ref[half:], "nn")
    whole_ref[...] = x_ref[...]
    out_ref[:, 0, :] = static_ref[...] - correction


def bound(body, *settings):
    def kernel(*refs):
        body(*settings, *refs)

    return kernel


def on_device(front, diag_inverse, load, panel_order, tie, mass, modes):
    vectors = load.shape[0]
    block = diag_inverse.shape[1]
    rows, half = front.shape
    half_panels = half // block
    plane = lax.axis_size(PLANE)
    depth = lax.axis_size("z")
    cores = lax.axis_size("k")
    mode_rows = modes.reshape(modes.shape[0], -1)

    small = ((vectors, half), F32)
    narrow = ((vectors, half), BF16)
    to_plane = ((plane, vectors, half), BF16)
    to_depth = ((depth, vectors, half), BF16)
    inverse_half = ((half_panels, block, block), BF16)

    def exchange(value, axes):
        return lax.all_to_all(value, axes, 0, 0, tiled=True)

    def both_cores(value):
        return lax.all_gather(value, "k", axis=0)

    level_row, high, low, mine, y, send, front = call(
        start_kernel,
        [((vectors, half), jnp.int32), inverse_half, inverse_half, small, small, to_plane, (front.shape, BF16)],
        Far(panel_order[None, :]), Far(load), Far(diag_inverse), Far(front),
        scratch=[
            pltpu.VMEM((1, panel_order.shape[0]), jnp.int32),
            pltpu.VMEM((half_panels, block, block), F32),
            pltpu.SemaphoreType.DMA((4,)),
        ],
    )
    pending = ()
    for level in range(1, LEVELS):
        got = exchange(send, PLANE)
        pending = tuple(call(update_kernel, [((vectors, rows), F32)], front, got, *pending))
        (send,) = call(pair_kernel, [to_depth], both_cores(pending[0]))
        got = exchange(send, "z")
        args = (got, mine, level_row, high, low, y)
        if level < LEVELS - 1:
            y, send = call(bound(forward_kernel, level), [small, to_plane], *args)
        else:
            y, x, fresh, mode_rows = call(
                turn_kernel,
                [small, small, narrow, (mode_rows.shape, BF16)],
                *args, Far(mode_rows),
                scratch=[pltpu.SemaphoreType.DMA(())],
            )

    pending = ()
    for level in reversed(range(LEVELS - 1)):
        last = level == 0
        *pending, send = call(
            bound(back_update_kernel, not pending, last),
            [to_plane] if last else [small, to_plane],
            front, both_cores(fresh), *pending,
        )
        got = exchange(send, PLANE)
        (send,) = call(bound(back_kernel, level), [to_depth], got, level_row, high, low, y)
        got = exchange(send, "z")
        if level > 0:
            x, fresh = call(pick_kernel, [small, narrow], got, x)
        else:
            (x,) = call(last_pick_kernel, [small], got, x)

    whole, static, send = call(
        coords_kernel,
        [((vectors, rows), F32), ((vectors, rows), F32), ((plane * cores, vectors, half), BF16)],
        both_cores(x), tie, mass, mode_rows,
    )
    (send,) = call(relay_kernel, [to_depth], exchange(send, PLANE + ("k",)))
    (coords,) = call(gathered_kernel, [narrow], exchange(send, "z"))
    return tuple(
        call(
            finish_kernel,
            [jax.ShapeDtypeStruct((vectors, rows), F32), jax.ShapeDtypeStruct((vectors, 1, rows), F32)],
            static, both_cores(coords), mode_rows, whole,
        )
    )


def solution(mesh):
    grid = Mesh(mesh.devices.reshape(4, 4, 16, 2), PLANE + ("z", "k"))
    row, col = PLANE, ("z", "k")
    in_specs = (
        P(row, col),
        P(row, None, None),
        P(None, row),
        P(),
        P(col, row),
        P(col, row),
        P(None, col, row),
    )
    out_specs = (P(None, row), P(None, col, row))
    return jax.shard_map(
        on_device, mesh=grid, in_specs=in_specs, out_specs=out_specs, check_vma=False
    )
```

time: 259 us -> 247 us (0.954)
  blocking collectives: 151 us -> 237 us
  waiting for transfers between devices: 54.7 us -> 0 us
  starting transfers between devices: 32.2 us -> 0 us
  matrix products: 13.3 us -> 0 us
  Pallas kernels: 0 us -> 7.87 us
  local copies, waits for them, and re-layouts: 4.5 us -> 0.02 us
    all_to_all x9 -> x14, blocking collectives: 105 us -> 195 us  [exchange(): return lax.all_to_all(value, axes, 0, 0, tiled=True)]
    all_to_all x5 -> x0, waiting for transfers between devices: 54.7 us -> none  [spread(): lax.all_to_all(jnp.broadcast_to(value[None], (count,) + value.shape), axe...]
    all_to_all x5 -> x0, starting transfers between devices: 32.2 us -> none  [spread(): lax.all_to_all(jnp.broadcast_to(value[None], (count,) + value.shape), axe...]
    dot_general x16 -> x0, matrix products: 13.3 us -> none  [the longest x8 9.22 us: solve(): jnp.einsum(form, value, inverse, precision=highest).reshape(vectors, half)]
    pallas_call x0 -> x23, Pallas kernels: none -> 7.87 us  [call(): pl.pallas_call(body, out_shape=[out if isinstance(out, jax.ShapeDtypeStru...]
    all_gather x9 -> x8, blocking collectives: 46.4 us -> 42.6 us  [both_cores(): return lax.all_gather(value, 'k', axis=0)]
    broadcast_in_dim x14 -> x0, local copies, waits for them, and re-layouts: 3.5 us -> none  [spread(): jnp.broadcast_to(value[None], (count,) + value.shape)]
  transfers between devices with their start and end apart: 5 -> 0, of which waited for: 5 -> 0; matrix products, arithmetic and copies ran while one was open for 0% -> 0% of each run, Pallas kernels for 0% -> 0%
where the time goes in v2:
time: 247 us; the launch traced here: 246 us
  blocking collectives  237 us (96%)
  Pallas kernels  7.87 us (3%)
    all_to_all x14, blocking collectives, exchange(): return lax.all_to_all(value, axes, 0, 0, tiled=True)  195 us
    all_gather x8, blocking collectives, both_cores(): return lax.all_gather(value, 'k', axis=0)  42.6 us
    pallas_call x23, Pallas kernels, call(): pl.pallas_call(body, out_shape=[out if isinstance(out, jax.ShapeDtypeStru...  7.87 us

profile of v2, /device:TPU:1, one launch (start us, length us, event | category | flops | bytes accessed | tf_op | source)
XLA Modules:
  0.0 246.1 jit_solution(16144628439728280340)
XLA Ops:
  0.6 1.4 shard_map.86
  2.0 14.1 %all_to_all.70.got_ref = bf16[16,8,512]{2,1,0:T(8,128)(2,1)S(1)} all-to-all(bf16[16,8,512]{2,1,0:T(8,128)(2,1)S(1)} %get-tuple-element.29), channel_id=1, replica_groups=mesh['x'=4,'y'=4,'z'=16,'k'=2] {'x','y'}, dimensions={0} | all-to-all | bytes 262144 | tf_op jit(solution)/shard_map/all_to_all | solution.py:225
  16.5 4.6 %all-gather = f32[16,1024]{1,0:T(8,128)S(1)} all-gather(f32[8,1024]{1,0:T(8,128)S(1)} %shard_map.87.refs_0_), channel_id=2, replica_groups=mesh['x'=4,'y'=4,'z'=16,'k'=2] {'k'}, dimensions={0}, use_global_device_ids=true | all-gather | bytes 98304 | tf_op jit(solution)/shard_map/all_gather | solution.py:228
  21.2 25.7 %all_to_all.71.refs_0_ = bf16[16,8,512]{2,1,0:T(8,128)(2,1)S(1)} all-to-all(bf16[16,8,512]{2,1,0:T(8,128)(2,1)S(1)} %shard_map.88), channel_id=1, replica_groups=mesh['x'=4,'y'=4,'z'=16,'k'=2] {'z'}, dimensions={0} | all-to-all | bytes 262144 | tf_op jit(solution)/shard_map/all_to_all | solution.py:225
  47.2 9.8 %all_to_all.72.got_ref = bf16[16,8,512]{2,1,0:T(8,128)(2,1)S(1)} all-to-all(bf16[16,8,512]{2,1,0:T(8,128)(2,1)S(1)} %get-tuple-element.35), channel_id=1, replica_groups=mesh['x'=4,'y'=4,'z'=16,'k'=2] {'x','y'}, dimensions={0} | all-to-all | bytes 262144 | tf_op jit(solution)/shard_map/all_to_all | solution.py:225
  57.4 6.2 %all-gather.1 = f32[16,1024]{1,0:T(8,128)S(1)} all-gather(f32[8,1024]{1,0:T(8,128)S(1)} %shard_map.90.refs_0_), channel_id=3, replica_groups=mesh['x'=4,'y'=4,'z'=16,'k'=2] {'k'}, dimensions={0}, use_global_device_ids=true | all-gather | bytes 98304 | tf_op jit(solution)/shard_map/all_gather | solution.py:228
  63.6 15.7 %all_to_all.73.refs_0_ = bf16[16,8,512]{2,1,0:T(8,128)(2,1)S(1)} all-to-all(bf16[16,8,512]{2,1,0:T(8,128)(2,1)S(1)} %shard_map.91), channel_id=1, replica_groups=mesh['x'=4,'y'=4,'z'=16,'k'=2] {'z'}, dimensions={0} | all-to-all | bytes 262144 | tf_op jit(solution)/shard_map/all_to_all | solution.py:225
  79.7 9.8 %all_to_all.74.got_ref = bf16[16,8,512]{2,1,0:T(8,128)(2,1)S(1)} all-to-all(bf16[16,8,512]{2,1,0:T(8,128)(2,1)S(1)} %get-tuple-element.37), channel_id=1, replica_groups=mesh['x'=4,'y'=4,'z'=16,'k'=2] {'x','y'}, dimensions={0} | all-to-all | bytes 262144 | tf_op jit(solution)/shard_map/all_to_all | solution.py:225
  89.8 6.2 %all-gather.2 = f32[16,1024]{1,0:T(8,128)S(1)} all-gather(f32[8,1024]{1,0:T(8,128)S(1)} %shard_map.93), channel_id=4, replica_groups=mesh['x'=4,'y'=4,'z'=16,'k'=2] {'k'}, dimensions={0}, use_global_device_ids=true | all-gather | bytes 98304 | tf_op jit(solution)/shard_map/all_gather | solution.py:228
  96.1 15.7 %all_to_all.75.got_ref = bf16[16,8,512]{2,1,0:T(8,128)(2,1)S(1)} all-to-all(bf16[16,8,512]{2,1,0:T(8,128)(2,1)S(1)} %shard_map.94), channel_id=1, replica_groups=mesh['x'=4,'y'=4,'z'=16,'k'=2] {'z'}, dimensions={0} | all-to-all | bytes 262144 | tf_op jit(solution)/shard_map/all_to_all | solution.py:225
  111.8 1.6 shard_map.95
  113.4 4.8 %all-gather.3 = bf16[16,512]{1,0:T(8,128)(2,1)S(1)} all-gather(bf16[8,512]{1,0:T(8,128)(2,1)S(1)} %get-tuple-element.39), channel_id=5, replica_groups=mesh['x'=4,'y'=4,'z'=16,'k'=2] {'k'}, dimensions={0}, use_global_device_ids=true | all-gather | bytes 24576 | tf_op jit(solution)/shard_map/all_gather | solution.py:228
  118.4 9.8 %all_to_all.76.refs_0_ = bf16[16,8,512]{2,1,0:T(8,128)(2,1)S(1)} all-to-all(bf16[16,8,512]{2,1,0:T(8,128)(2,1)S(1)} %get-tuple-element.40), channel_id=1, replica_groups=mesh['x'=4,'y'=4,'z'=16,'k'=2] {'x','y'}, dimensions={0} | all-to-all | bytes 262144 | tf_op jit(solution)/shard_map/all_to_all | solution.py:225
  128.5 15.6 %all_to_all.77.got_ref = bf16[16,8,512]{2,1,0:T(8,128)(2,1)S(1)} all-to-all(bf16[16,8,512]{2,1,0:T(8,128)(2,1)S(1)} %shard_map.97), channel_id=1, replica_groups=mesh['x'=4,'y'=4,'z'=16,'k'=2] {'z'}, dimensions={0} | all-to-all | bytes 262144 | tf_op jit(solution)/shard_map/all_to_all | solution.py:225
  144.1 5.5 %all-gather.4 = bf16[16,512]{1,0:T(8,128)(2,1)S(1)} all-gather(bf16[8,512]{1,0:T(8,128)(2,1)S(1)} %get-tuple-element.43), channel_id=6, replica_groups=mesh['x'=4,'y'=4,'z'=16,'k'=2] {'k'}, dimensions={0}, use_global_device_ids=true | all-gather | bytes 24576 | tf_op jit(solution)/shard_map/all_gather | solution.py:228
  149.8 10.0 %all_to_all.78.refs_0_ = bf16[16,8,512]{2,1,0:T(8,128)(2,1)S(1)} all-to-all(bf16[16,8,512]{2,1,0:T(8,128)(2,1)S(1)} %get-tuple-element.45), channel_id=1, replica_groups=mesh['x'=4,'y'=4,'z'=16,'k'=2] {'x','y'}, dimensions={0} | all-to-all | bytes 262144 | tf_op jit(solution)/shard_map/all_to_all | solution.py:225
  160.0 15.3 %all_to_all.79.got_ref = bf16[16,8,512]{2,1,0:T(8,128)(2,1)S(1)} all-to-all(bf16[16,8,512]{2,1,0:T(8,128)(2,1)S(1)} %shard_map.100), channel_id=1, replica_groups=mesh['x'=4,'y'=4,'z'=16,'k'=2] {'z'}, dimensions={0} | all-to-all | bytes 262144 | tf_op jit(solution)/shard_map/all_to_all | solution.py:225
  175.3 5.5 %all-gather.5 = bf16[16,512]{1,0:T(8,128)(2,1)S(1)} all-gather(bf16[8,512]{1,0:T(8,128)(2,1)S(1)} %get-tuple-element.47), channel_id=7, replica_groups=mesh['x'=4,'y'=4,'z'=16,'k'=2] {'k'}, dimensions={0}, use_global_device_ids=true | all-gather | bytes 24576 | tf_op jit(solution)/shard_map/all_gather | solution.py:228
  181.0 9.8 %all_to_all.80.refs_0_ = bf16[16,8,512]{2,1,0:T(8,128)(2,1)S(1)} all-to-all(bf16[16,8,512]{2,1,0:T(8,128)(2,1)S(1)} %shard_map.102), channel_id=1, replica_groups=mesh['x'=4,'y'=4,'z'=16,'k'=2] {'x','y'}, dimensions={0} | all-to-all | bytes 262144 | tf_op jit(solution)/shard_map/all_to_all | solution.py:225
  191.0 15.3 %all_to_all.81.got_ref = bf16[16,8,512]{2,1,0:T(8,128)(2,1)S(1)} all-to-all(bf16[16,8,512]{2,1,0:T(8,128)(2,1)S(1)} %shard_map.103), channel_id=1, replica_groups=mesh['x'=4,'y'=4,'z'=16,'k'=2] {'z'}, dimensions={0} | all-to-all | bytes 262144 | tf_op jit(solution)/shard_map/all_to_all | solution.py:225
  206.3 5.5 %all-gather.6 = f32[16,512]{1,0:T(8,128)S(1)} all-gather(f32[8,512]{1,0:T(8,128)S(1)} %shard_map.104), channel_id=8, replica_groups=mesh['x'=4,'y'=4,'z'=16,'k'=2] {'k'}, dimensions={0}, use_global_device_ids=true | all-gather | bytes 49152 | tf_op jit(solution)/shard_map/all_gather | solution.py:228
  212.5 12.8 %all_to_all.82.got_ref = bf16[32,8,512]{2,1,0:T(8,128)(2,1)S(1)} all-to-all(bf16[32,8,512]{2,1,0:T(8,128)(2,1)S(1)} %get-tuple-element.52), channel_id=1, replica_groups=mesh['x'=4,'y'=4,'z'=16,'k'=2] {'x','y','k'}, dimensions={0} | all-to-all | bytes 524288 | tf_op jit(solution)/shard_map/all_to_all | solution.py:225
  225.3 15.4 %all_to_all.83.got_ref = bf16[16,8,512]{2,1,0:T(8,128)(2,1)S(1)} all-to-all(bf16[16,8,512]{2,1,0:T(8,128)(2,1)S(1)} %shard_map.106), channel_id=1, replica_groups=mesh['x'=4,'y'=4,'z'=16,'k'=2] {'z'}, dimensions={0} | all-to-all | bytes 262144 | tf_op jit(solution)/shard_map/all_to_all | solution.py:225
  240.7 4.3 %all-gather.7 = bf16[16,512]{1,0:T(8,128)(2,1)S(1)} all-gather(bf16[8,512]{1,0:T(8,128)(2,1)S(1)} %shard_map.107), channel_id=9, replica_groups=mesh['x'=4,'y'=4,'z'=16,'k'=2] {'k'}, dimensions={0}, use_global_device_ids=true | all-gather | bytes 24576 | tf_op jit(solution)/shard_map/all_gather | solution.py:228
  (25 shorter events, 4.9 us)
Async XLA Ops:
  149.8 62.0 %copy-start = (f32[1,1024]{1,0:T(1,128)S(1)}, f32[1,1024]{1,0:T(1,128)}, u32[]{:S(2)}) copy-start(f32[1,1024]{1,0:T(1,128)} %tie_ref.1) | copy-start | bytes 12292
  149.8 62.0 %copy-start.1 = (f32[1,1024]{1,0:T(1,128)S(1)}, f32[1,1024]{1,0:T(1,128)}, u32[]{:S(2)}) copy-start(f32[1,1024]{1,0:T(1,128)} %mass_ref.1) | copy-start | bytes 12292

commit v3 on v2

v3 whole, which is shorter than its diff:
```python
import jax
import jax.numpy as jnp
from jax import lax
from jax.experimental import pallas as pl
from jax.experimental.pallas import tpu as pltpu
from jax.sharding import Mesh, PartitionSpec as P

LEVELS = 4
PLANE = ("x", "y")
F32, BF16 = jnp.float32, jnp.bfloat16


def matmul(a, b, form):
    dims = {"nn": (((1,), (0,)), ((), ())), "nt": (((1,), (1,)), ((), ()))}[form]
    return lax.dot_general(a, b, dims, preferred_element_type=F32)


def split(value):
    high = value.astype(BF16)
    return high, (value - high.astype(F32)).astype(BF16)


class Far:
    def __init__(self, array):
        self.array = array


def call(body, outs, *args, scratch=()):
    vmem = pl.BlockSpec(memory_space=pltpu.VMEM)
    in_specs, given = [], []
    for arg in args:
        if isinstance(arg, Far):
            in_specs.append(pl.BlockSpec(memory_space=pltpu.HBM))
            given.append(pltpu.with_memory_space_constraint(arg.array, pltpu.HBM))
        else:
            in_specs.append(vmem)
            given.append(pltpu.with_memory_space_constraint(arg, pltpu.VMEM))
    return pl.pallas_call(
        body,
        out_shape=[out if isinstance(out, jax.ShapeDtypeStruct) else pltpu.VMEM(*out) for out in outs],
        in_specs=in_specs,
        out_specs=[vmem] * len(outs),
        scratch_shapes=list(scratch),
        compiler_params=pltpu.CompilerParams(vmem_limit_bytes=8 << 20),
    )(*given)


def send_to_all(out_ref, value):
    value = value.astype(BF16)
    for slot in range(out_ref.shape[0]):
        out_ref[slot] = value


def sum_slots(ref):
    total = ref[0].astype(F32)
    for slot in range(1, ref.shape[0]):
        total = total + ref[slot].astype(F32)
    return total


def packed(value):
    half = value.shape[1] // 2
    return jnp.concatenate([value[:, :half], value[:, half:]], axis=0)


def unpacked(value):
    rows = value.shape[0] // 2
    return jnp.concatenate([value[:rows], value[rows:]], axis=1)


def solve(value, high_ref, low_ref, form):
    rows, block = value.shape[0], high_ref.shape[1]
    out = []
    for p in range(high_ref.shape[0]):
        panel = value[:, p * block : (p + 1) * block]
        top = panel.astype(BF16).astype(F32)
        both = jnp.concatenate([top, panel - top], axis=0).astype(BF16)
        product = matmul(both, high_ref[p], form) + matmul(both, low_ref[p], form)
        out.append(product[:rows] + product[rows:])
    return jnp.concatenate(out, axis=1)


def start_kernel(
    order_hbm, load_hbm, inverse_hbm, front_hbm, modes_hbm,
    level_ref, high_ref, low_ref, mine_ref, y_ref, send_ref, front_ref, modes_ref,
    order_ref, load_ref, inverse_ref, sems,
):
    panels, block = high_ref.shape[0], high_ref.shape[1]
    vectors = load_ref.shape[0] // 2
    copies = [
        pltpu.make_async_copy(order_hbm, order_ref, sems.at[0]),
        pltpu.make_async_copy(load_hbm, load_ref, sems.at[1]),
        pltpu.make_async_copy(inverse_hbm, inverse_ref, sems.at[2]),
        pltpu.make_async_copy(front_hbm, front_ref, sems.at[3]),
        pltpu.make_async_copy(modes_hbm, modes_ref, sems.at[4]),
    ]
    for copy in copies:
        copy.start()
    copies[0].wait()
    order = jnp.broadcast_to(order_ref[...], (panels, order_ref.shape[1]))
    per_level = order.shape[1] // LEVELS
    names = lax.axis_index(PLANE) * panels + lax.broadcasted_iota(jnp.int32, order.shape, 0)
    counting = lax.broadcasted_iota(jnp.int32, order.shape, 1)
    ranks = jnp.sum(jnp.where(order == names, counting, 0), axis=1, keepdims=True)
    levels = jnp.zeros_like(ranks)
    for bound in range(1, LEVELS):
        levels = levels + jnp.where(ranks >= bound * per_level, 1, 0)
    levels = jnp.broadcast_to(levels, (panels, block))
    level_row = jnp.concatenate(
        [jnp.broadcast_to(levels[p : p + 1], (vectors, block)) for p in range(panels)], axis=1
    )
    level_ref[...] = level_row
    copies[1].wait()
    load = jnp.where(lax.axis_index("k") == 0, load_ref[:vectors], load_ref[vectors:])
    mine_ref[...] = load
    copies[2].wait()
    high, low = split(inverse_ref[...])
    high_ref[...] = high
    low_ref[...] = low
    y = jnp.where(level_row == 0, solve(load, high_ref, low_ref, "nt"), 0.0)
    y_ref[...] = y
    send_to_all(send_ref, packed(y))
    copies[3].wait()
    copies[4].wait()


def update_kernel(first, last, front_ref, partner_ref, got_ref, *refs):
    got = got_ref[lax.axis_index("z")]
    rows = got.shape[0] // 2
    own, other = matmul(got, front_ref[...], "nt"), matmul(got, partner_ref[...], "nt")
    out = jnp.where(lax.axis_index("k") == 0, own[:rows] + other[rows:], own[rows:] + other[:rows])
    if not first:
        out = refs[0][...] + out
    if not last:
        refs[-2][...] = out
    send_to_all(refs[-1], packed(out))


def forward_kernel(level, got_ref, mine_ref, level_ref, high_ref, low_ref, y_in_ref, y_ref, send_ref):
    chosen = level_ref[...] == level
    candidate = solve(mine_ref[...] - unpacked(sum_slots(got_ref)), high_ref, low_ref, "nt")
    y_ref[...] = jnp.where(chosen, candidate, y_in_ref[...])
    send_to_all(send_ref, packed(jnp.where(chosen, candidate, 0.0)))


def back_product(x, front_ref, partner_ref):
    x = x.astype(BF16)
    own, other = matmul(x, front_ref[...], "nn"), matmul(x, partner_ref[...], "nn")
    first = lax.axis_index("k") == 0
    return jnp.concatenate([jnp.where(first, own, other), jnp.where(first, other, own)], axis=0)


def turn_kernel(
    front_ref, partner_ref, got_ref, mine_ref, level_ref, high_ref, low_ref, y_in_ref,
    y_ref, x_ref, pending_ref, send_ref,
):
    chosen = level_ref[...] == LEVELS - 1
    candidate = solve(mine_ref[...] - unpacked(sum_slots(got_ref)), high_ref, low_ref, "nt")
    y = jnp.where(chosen, candidate, y_in_ref[...])
    y_ref[...] = y
    x = jnp.where(chosen, solve(y, high_ref, low_ref, "nn"), 0.0)
    x_ref[...] = packed(x)
    out = back_product(x, front_ref, partner_ref)
    pending_ref[...] = out
    send_to_all(send_ref, out)


def back_kernel(level, got_ref, level_ref, high_ref, low_ref, y_ref, send_ref):
    x = solve(y_ref[...] - unpacked(sum_slots(got_ref)), high_ref, low_ref, "nn")
    send_to_all(send_ref, packed(jnp.where(level_ref[...] == level, x, 0.0)))


def back_update_kernel(last, front_ref, partner_ref, got_ref, x_in_ref, pending_in_ref, x_ref, *refs):
    fresh = got_ref[lax.axis_index(PLANE)].astype(F32)
    x_ref[...] = x_in_ref[...] + fresh
    out = pending_in_ref[...] + back_product(unpacked(fresh), front_ref, partner_ref)
    if not last:
        refs[0][...] = out
    send_to_all(refs[-1], out)


def last_pick_kernel(got_ref, x_in_ref, x_ref):
    x_ref[...] = x_in_ref[...] + got_ref[lax.axis_index(PLANE)].astype(F32)


def coords_kernel(pair_ref, tie_ref, mass_ref, modes_ref, x_ref, static_ref, send_ref):
    x = jnp.concatenate([unpacked(pair_ref[0]), unpacked(pair_ref[1])], axis=0)
    x_ref[...] = x
    static = tie_ref[...] * x
    static_ref[...] = static
    coords = matmul((mass_ref[...] * static).astype(BF16), modes_ref[...], "nt").astype(BF16)
    cores, half = 2, send_ref.shape[2]
    for slot in range(send_ref.shape[0]):
        part = slot % cores
        send_ref[slot] = coords[:, part * half : (part + 1) * half]


def relay_kernel(got_ref, send_ref):
    send_to_all(send_ref, sum_slots(got_ref))


def gathered_kernel(got_ref, out_ref):
    out_ref[...] = sum_slots(got_ref).astype(BF16)


def finish_kernel(static_ref, pair_ref, modes_ref, x_ref, whole_ref, out_ref):
    half = pair_ref.shape[2]
    correction = matmul(pair_ref[0], modes_ref[:half], "nn") + matmul(pair_ref[1], modes_ref[half:], "nn")
    whole_ref[...] = x_ref[...]
    out_ref[:, 0, :] = static_ref[...] - correction


def bound(body, *settings):
    def kernel(*refs):
        body(*settings, *refs)

    return kernel


def on_device(front, diag_inverse, load, panel_order, tie, mass, modes):
    vectors = load.shape[0]
    rows, half = front.shape
    plane = lax.axis_size(PLANE)
    depth = lax.axis_size("z")
    cores = lax.axis_size("k")
    mode_rows = modes.reshape(modes.shape[0], -1)

    flat = (vectors // cores, rows)
    small = ((vectors, half), F32)
    narrow = ((vectors, half), BF16)
    to_plane = ((plane, vectors, half), BF16)
    to_depth = ((depth, vectors, half), BF16)
    inverse_part = (diag_inverse.shape, BF16)

    def exchange(value, axes):
        return lax.all_to_all(value, axes, 0, 0, tiled=True)

    def both_cores(value):
        return lax.all_gather(value, "k", axis=0)

    partner = lax.ppermute(front, "k", [(core, 1 - core) for core in range(cores)])
    level_row, high, low, mine, y, send, front, mode_rows = call(
        start_kernel,
        [(flat, jnp.int32), inverse_part, inverse_part, (flat, F32), (flat, F32), to_plane,
         (front.shape, BF16), (mode_rows.shape, BF16)],
        Far(panel_order[None, :]), Far(load), Far(diag_inverse), Far(front), Far(mode_rows),
        scratch=[
            pltpu.VMEM((1, panel_order.shape[0]), jnp.int32),
            pltpu.VMEM(load.shape, F32),
            pltpu.VMEM(diag_inverse.shape, F32),
            pltpu.SemaphoreType.DMA((5,)),
        ],
    )
    pending = ()
    for level in range(1, LEVELS):
        last = level == LEVELS - 1
        *pending, send = call(
            bound(update_kernel, not pending, last),
            [to_depth] if last else [(flat, F32), to_depth],
            front, partner, exchange(send, PLANE), *pending,
        )
        args = (exchange(send, "z"), mine, level_row, high, low, y)
        if not last:
            y, send = call(bound(forward_kernel, level), [(flat, F32), to_plane], *args)
    y, x, pending, send = call(turn_kernel, [(flat, F32), small, small, to_plane], front, partner, *args)

    for level in reversed(range(LEVELS - 1)):
        (send,) = call(bound(back_kernel, level), [to_depth], exchange(send, PLANE), level_row, high, low, y)
        got = exchange(send, "z")
        if level > 0:
            last = level == 1
            x, *rest, send = call(
                bound(back_update_kernel, last),
                [small, to_plane] if last else [small, small, to_plane],
                front, partner, got, x, pending,
            )
            pending = None if last else rest[0]
        else:
            (x,) = call(last_pick_kernel, [small], got, x)

    whole, static, send = call(
        coords_kernel,
        [((vectors, rows), F32), ((vectors, rows), F32), ((plane * cores, vectors, half), BF16)],
        both_cores(x), tie, mass, mode_rows,
    )
    (send,) = call(relay_kernel, [to_depth], exchange(send, PLANE + ("k",)))
    (coords,) = call(gathered_kernel, [narrow], exchange(send, "z"))
    return tuple(
        call(
            finish_kernel,
            [jax.ShapeDtypeStruct((vectors, rows), F32), jax.ShapeDtypeStruct((vectors, 1, rows), F32)],
            static, both_cores(coords), mode_rows, whole,
        )
    )


def solution(mesh):
    grid = Mesh(mesh.devices.reshape(4, 4, 16, 2), PLANE + ("z", "k"))
    row, col = PLANE, ("z", "k")
    in_specs = (
        P(row, col),
        P(row, None, None),
        P(None, row),
        P(),
        P(col, row),
        P(col, row),
        P(None, col, row),
    )
    out_specs = (P(None, row), P(None, col, row))
    return jax.shard_map(
        on_device, mesh=grid, in_specs=in_specs, out_specs=out_specs, check_vma=False
    )
```

time: 247 us -> 233 us (0.943)
  blocking collectives: 237 us -> 213 us
  starting transfers between devices: 0 us -> 8.75 us
    all_gather x8 -> x2, blocking collectives: 42.6 us -> 20.5 us  [both_cores(): return lax.all_gather(value, 'k', axis=0)]
    ppermute x0 -> x1, starting transfers between devices: none -> 8.75 us  [on_device(): lax.ppermute(front, 'k', [(core, 1 - core) for core in range(cores)])]
    pallas_call x23 -> x17, Pallas kernels: 7.87 us -> 9.09 us  [call(): pl.pallas_call(body, out_shape=[out if isinstance(out, jax.ShapeDtypeStru...]
  transfers between devices with their start and end apart: 0 -> 1, of which waited for: 0 -> 0; matrix products, arithmetic and copies ran while one was open for 0% -> 0% of each run, Pallas kernels for 0% -> 1%
where the time goes in v3:
time: 233 us; the launch traced here: 232 us
  blocking collectives  213 us (91%)
  Pallas kernels  9.09 us (4%)
  starting transfers between devices  8.75 us (4%)
    all_to_all x14, blocking collectives, exchange(): return lax.all_to_all(value, axes, 0, 0, tiled=True)  193 us
    all_gather x2, blocking collectives, both_cores(): return lax.all_gather(value, 'k', axis=0)  20.5 us
    pallas_call x17, Pallas kernels, call(): pl.pallas_call(body, out_shape=[out if isinstance(out, jax.ShapeDtypeStru...  9.09 us
    ppermute x1, starting transfers between devices, on_device(): lax.ppermute(front, 'k', [(core, 1 - core) for core in range(cores)])  8.75 us
  transfers between devices with their start and end apart: 1, of which 0 were waited for; matrix products, arithmetic and copies ran while one was open for 0% of the time, Pallas kernels for 1%

profile of v3, /device:TPU:1, one launch (start us, length us, event | category | flops | bytes accessed | tf_op | source)
XLA Modules:
  0.0 232.1 jit_solution(18436485106766098902)
XLA Ops:
  0.6 8.7 %collective-permute-start = (bf16[1024,512]{1,0:T(8,128)(2,1)}, bf16[1024,512]{1,0:T(8,128)(2,1)S(1)}, u32[]{:S(2)}, u32[]{:S(2)}) collective-permute-start(bf16[1024,512]{1,0:T(8,128)(2,1)} %front_hbm.1), channel_id=1, source_target_pairs={{0,1},{1,0},{2,3},{3,2},{4,5},{5,4},{6,7},{7,6},{8,9},{9,8},{10,11... | collective-permute-start | bytes 3145736 | tf_op jit(solution)/shard_map/ppermute | solution.py:241
  9.4 2.2 shard_map.86
  11.5 9.3 %all_to_all.70.refs_2_ = bf16[16,8,512]{2,1,0:T(8,128)(2,1)S(1)} all-to-all(bf16[16,8,512]{2,1,0:T(8,128)(2,1)S(1)} %get-tuple-element.31), channel_id=1, replica_groups=mesh['x'=4,'y'=4,'z'=16,'k'=2] {'x','y'}, dimensions={0} | all-to-all | bytes 262144 | tf_op jit(solution)/shard_map/all_to_all | solution.py:236
  20.9 0.7 shard_map.87
  21.6 25.3 %all_to_all.71.refs_0_ = bf16[16,8,512]{2,1,0:T(8,128)(2,1)S(1)} all-to-all(bf16[16,8,512]{2,1,0:T(8,128)(2,1)S(1)} %get-tuple-element.32), channel_id=1, replica_groups=mesh['x'=4,'y'=4,'z'=16,'k'=2] {'z'}, dimensions={0} | all-to-all | bytes 262144 | tf_op jit(solution)/shard_map/all_to_all | solution.py:236
  47.2 10.1 %all_to_all.72.refs_2_ = bf16[16,8,512]{2,1,0:T(8,128)(2,1)S(1)} all-to-all(bf16[16,8,512]{2,1,0:T(8,128)(2,1)S(1)} %get-tuple-element.38), channel_id=1, replica_groups=mesh['x'=4,'y'=4,'z'=16,'k'=2] {'x','y'}, dimensions={0} | all-to-all | bytes 262144 | tf_op jit(solution)/shard_map/all_to_all | solution.py:236
  57.3 0.7 shard_map.89
  58.0 17.4 %all_to_all.73.refs_0_ = bf16[16,8,512]{2,1,0:T(8,128)(2,1)S(1)} all-to-all(bf16[16,8,512]{2,1,0:T(8,128)(2,1)S(1)} %get-tuple-element.40), channel_id=1, replica_groups=mesh['x'=4,'y'=4,'z'=16,'k'=2] {'z'}, dimensions={0} | all-to-all | bytes 262144 | tf_op jit(solution)/shard_map/all_to_all | solution.py:236
  75.8 10.1 %all_to_all.74.refs_2_ = bf16[16,8,512]{2,1,0:T(8,128)(2,1)S(1)} all-to-all(bf16[16,8,512]{2,1,0:T(8,128)(2,1)S(1)} %get-tuple-element.42), channel_id=1, replica_groups=mesh['x'=4,'y'=4,'z'=16,'k'=2] {'x','y'}, dimensions={0} | all-to-all | bytes 262144 | tf_op jit(solution)/shard_map/all_to_all | solution.py:236
  85.9 0.7 shard_map.91
  86.6 15.9 %all_to_all.75.got_ref = bf16[16,8,512]{2,1,0:T(8,128)(2,1)S(1)} all-to-all(bf16[16,8,512]{2,1,0:T(8,128)(2,1)S(1)} %shard_map.91), channel_id=1, replica_groups=mesh['x'=4,'y'=4,'z'=16,'k'=2] {'z'}, dimensions={0} | all-to-all | bytes 262144 | tf_op jit(solution)/shard_map/all_to_all | solution.py:236
  102.4 0.8 shard_map.92
  103.3 9.8 %all_to_all.76.refs_0_ = bf16[16,8,512]{2,1,0:T(8,128)(2,1)S(1)} all-to-all(bf16[16,8,512]{2,1,0:T(8,128)(2,1)S(1)} %get-tuple-element.45), channel_id=1, replica_groups=mesh['x'=4,'y'=4,'z'=16,'k'=2] {'x','y'}, dimensions={0} | all-to-all | bytes 262144 | tf_op jit(solution)/shard_map/all_to_all | solution.py:236
  113.3 15.8 %all_to_all.77.refs_2_ = bf16[16,8,512]{2,1,0:T(8,128)(2,1)S(1)} all-to-all(bf16[16,8,512]{2,1,0:T(8,128)(2,1)S(1)} %shard_map.93), channel_id=1, replica_groups=mesh['x'=4,'y'=4,'z'=16,'k'=2] {'z'}, dimensions={0} | all-to-all | bytes 262144 | tf_op jit(solution)/shard_map/all_to_all | solution.py:236
  129.5 9.8 %all_to_all.78.refs_0_ = bf16[16,8,512]{2,1,0:T(8,128)(2,1)S(1)} all-to-all(bf16[16,8,512]{2,1,0:T(8,128)(2,1)S(1)} %get-tuple-element.49), channel_id=1, replica_groups=mesh['x'=4,'y'=4,'z'=16,'k'=2] {'x','y'}, dimensions={0} | all-to-all | bytes 262144 | tf_op jit(solution)/shard_map/all_to_all | solution.py:236
  139.6 15.5 %all_to_all.79.refs_2_ = bf16[16,8,512]{2,1,0:T(8,128)(2,1)S(1)} all-to-all(bf16[16,8,512]{2,1,0:T(8,128)(2,1)S(1)} %shard_map.95), channel_id=1, replica_groups=mesh['x'=4,'y'=4,'z'=16,'k'=2] {'z'}, dimensions={0} | all-to-all | bytes 262144 | tf_op jit(solution)/shard_map/all_to_all | solution.py:236
  155.5 10.1 %all_to_all.80.refs_0_ = bf16[16,8,512]{2,1,0:T(8,128)(2,1)S(1)} all-to-all(bf16[16,8,512]{2,1,0:T(8,128)(2,1)S(1)} %get-tuple-element.52), channel_id=1, replica_groups=mesh['x'=4,'y'=4,'z'=16,'k'=2] {'x','y'}, dimensions={0} | all-to-all | bytes 262144 | tf_op jit(solution)/shard_map/all_to_all | solution.py:236
  165.9 15.5 %all_to_all.81.got_ref = bf16[16,8,512]{2,1,0:T(8,128)(2,1)S(1)} all-to-all(bf16[16,8,512]{2,1,0:T(8,128)(2,1)S(1)} %shard_map.97), channel_id=1, replica_groups=mesh['x'=4,'y'=4,'z'=16,'k'=2] {'z'}, dimensions={0} | all-to-all | bytes 262144 | tf_op jit(solution)/shard_map/all_to_all | solution.py:236
  181.4 16.2 %all-gather = f32[16,512]{1,0:T(8,128)S(1)} all-gather(f32[8,512]{1,0:T(8,128)S(1)} %shard_map.98), channel_id=2, replica_groups=mesh['x'=4,'y'=4,'z'=16,'k'=2] {'k'}, dimensions={0}, use_global_device_ids=true | all-gather | bytes 49152 | tf_op jit(solution)/shard_map/all_gather | solution.py:239
  197.6 0.7 shard_map.99
  198.3 12.8 %all_to_all.82.got_ref = bf16[32,8,512]{2,1,0:T(8,128)(2,1)S(1)} all-to-all(bf16[32,8,512]{2,1,0:T(8,128)(2,1)S(1)} %get-tuple-element.56), channel_id=1, replica_groups=mesh['x'=4,'y'=4,'z'=16,'k'=2] {'x','y','k'}, dimensions={0} | all-to-all | bytes 524288 | tf_op jit(solution)/shard_map/all_to_all | solution.py:236
  211.1 15.7 %all_to_all.83.got_ref = bf16[16,8,512]{2,1,0:T(8,128)(2,1)S(1)} all-to-all(bf16[16,8,512]{2,1,0:T(8,128)(2,1)S(1)} %shard_map.100), channel_id=1, replica_groups=mesh['x'=4,'y'=4,'z'=16,'k'=2] {'z'}, dimensions={0} | all-to-all | bytes 262144 | tf_op jit(solution)/shard_map/all_to_all | solution.py:236
  226.8 4.3 %all-gather.1 = bf16[16,512]{1,0:T(8,128)(2,1)S(1)} all-gather(bf16[8,512]{1,0:T(8,128)(2,1)S(1)} %shard_map.101), channel_id=3, replica_groups=mesh['x'=4,'y'=4,'z'=16,'k'=2] {'k'}, dimensions={0}, use_global_device_ids=true | all-gather | bytes 24576 | tf_op jit(solution)/shard_map/all_gather | solution.py:239
  231.1 1.0 shard_map.102
  (15 shorter events, 2.5 us)
Async XLA Ops:
  0.6 20.3 %collective-permute-start = (bf16[1024,512]{1,0:T(8,128)(2,1)}, bf16[1024,512]{1,0:T(8,128)(2,1)S(1)}, u32[]{:S(2)}, u32[]{:S(2)}) collective-permute-start(bf16[1024,512]{1,0:T(8,128)(2,1)} %front_hbm.1), channel_id=1, source_target_pairs={{0,1},{1,0},{2,3},{3,2},{4,5},{5,4},{6,7},{7,6},{8,9},{9,8},{10,11... | collective-permute-start | bytes 3145736 | tf_op jit(solution)/shard_map/ppermute | solution.py:241
  139.6 58.0 %copy-start = (f32[1,1024]{1,0:T(1,128)S(1)}, f32[1,1024]{1,0:T(1,128)}, u32[]{:S(2)}) copy-start(f32[1,1024]{1,0:T(1,128)} %tie_ref.1) | copy-start | bytes 12292
  139.6 58.0 %copy-start.1 = (f32[1,1024]{1,0:T(1,128)S(1)}, f32[1,1024]{1,0:T(1,128)}, u32[]{:S(2)}) copy-start(f32[1,1024]{1,0:T(1,128)} %mass_ref.1) | copy-start | bytes 12292

commit v4 on v3

v4 whole, which is shorter than its diff:
```python
import jax
import jax.numpy as jnp
from jax import lax
from jax.experimental import pallas as pl
from jax.experimental.pallas import tpu as pltpu
from jax.sharding import Mesh, PartitionSpec as P


LEVELS = 4
ROOM = (4, 5, 6)
PLANE = ("x", "y")
F32, BF16 = jnp.float32, jnp.bfloat16


def matmul(a, b, form):
    dims = {"nn": (((1,), (0,)), ((), ())), "nt": (((1,), (1,)), ((), ()))}[form]
    return lax.dot_general(a, b, dims, preferred_element_type=F32)


def split(value):
    high = value.astype(BF16)
    return high, (value - high.astype(F32)).astype(BF16)


class Far:
    def __init__(self, array):
        self.array = array


def call(body, outs, *args, scratch=()):
    vmem = pl.BlockSpec(memory_space=pltpu.VMEM)
    in_specs, given = [], []
    for arg in args:
        if isinstance(arg, Far):
            in_specs.append(pl.BlockSpec(memory_space=pltpu.HBM))
            given.append(pltpu.with_memory_space_constraint(arg.array, pltpu.HBM))
        else:
            in_specs.append(vmem)
            given.append(pltpu.with_memory_space_constraint(arg, pltpu.VMEM))
    return pl.pallas_call(
        body,
        out_shape=[out if isinstance(out, jax.ShapeDtypeStruct) else pltpu.VMEM(*out) for out in outs],
        in_specs=in_specs,
        out_specs=[vmem] * len(outs),
        scratch_shapes=list(scratch),
        compiler_params=pltpu.CompilerParams(vmem_limit_bytes=8 << 20),
    )(*given)


def send_to_all(out_ref, value):
    value = value.astype(BF16)
    for slot in range(out_ref.shape[0]):
        out_ref[slot] = value


def sum_slots(ref):
    total = ref[0].astype(F32)
    for slot in range(1, ref.shape[0]):
        total = total + ref[slot].astype(F32)
    return total


def pick(value, code, first, room):
    block = 128
    panels = value.shape[1] // block
    out = []
    for j in range(room):
        total = None
        for p in range(panels):
            at = slice(p * block, (p + 1) * block)
            part = jnp.where(code[:, at] == first + j, value[:, at], 0.0)
            total = part if total is None else total + part
        out.append(total)
    return jnp.concatenate(out, axis=1)


def place(value, code, first, room):
    block = 128
    panels = code.shape[1] // block
    out = []
    for p in range(panels):
        at = slice(p * block, (p + 1) * block)
        total = jnp.zeros((code.shape[0], block), F32)
        for j in range(room):
            total = total + jnp.where(code[:, at] == first + j, value[:, j * block : (j + 1) * block], 0.0)
        out.append(total)
    return jnp.concatenate(out, axis=1)


def solve(value, high_ref, low_ref, form):
    rows, block = value.shape[0], high_ref.shape[1]
    out = []
    for p in range(high_ref.shape[0]):
        panel = value[:, p * block : (p + 1) * block]
        top = panel.astype(BF16).astype(F32)
        both = jnp.concatenate([top, panel - top], axis=0).astype(BF16)
        product = matmul(both, high_ref[p], form) + matmul(both, low_ref[p], form)
        out.append(product[:rows] + product[rows:])
    return jnp.concatenate(out, axis=1)


def in_level(code, level, panels):
    return (code >= level * panels) & (code < (level + 1) * panels)


def start_kernel(
    order_hbm, load_hbm, inverse_hbm, front_hbm,
    row_code_ref, col_code_ref, high_ref, low_ref, mine_ref, y_ref, send_ref, front_ref,
    order_ref, load_ref, inverse_ref, sems,
):
    panels, block = high_ref.shape[0], high_ref.shape[1]
    vectors = load_ref.shape[0] // 2
    copies = [
        pltpu.make_async_copy(order_hbm, order_ref, sems.at[0]),
        pltpu.make_async_copy(load_hbm, load_ref, sems.at[1]),
        pltpu.make_async_copy(inverse_hbm, inverse_ref, sems.at[2]),
        pltpu.make_async_copy(front_hbm, front_ref, sems.at[3]),
    ]
    for copy in copies:
        copy.start()
    copies[0].wait()
    order = jnp.broadcast_to(order_ref[...], (2 * panels, order_ref.shape[1]))
    per_level = order.shape[1] // LEVELS
    panel = lax.broadcasted_iota(jnp.int32, order.shape, 0)
    of_rows = panel < panels
    place_in = jnp.where(of_rows, panel, panel - panels)
    names = jnp.where(of_rows, lax.axis_index(PLANE), lax.axis_index("z")) * panels + place_in
    counting = lax.broadcasted_iota(jnp.int32, order.shape, 1)
    ranks = jnp.sum(jnp.where(order == names, counting, 0), axis=1, keepdims=True)
    levels = jnp.zeros_like(ranks)
    for bound in range(1, LEVELS):
        levels = levels + jnp.where(ranks >= bound * per_level, 1, 0)
    levels = jnp.broadcast_to(levels, order.shape)
    codes = levels * panels
    for p in range(panels - 1):
        same = levels == jnp.where(of_rows, levels[p : p + 1], levels[panels + p : panels + p + 1])
        codes = codes + jnp.where(same & (place_in > p), 1, 0)
    spread_codes = [jnp.broadcast_to(codes[p : p + 1], (vectors, block)) for p in range(2 * panels)]
    row_code = jnp.concatenate(spread_codes[:panels], axis=1)
    row_code_ref[...] = row_code
    col_code_ref[...] = jnp.concatenate(spread_codes[panels:], axis=1)
    copies[1].wait()
    load = jnp.where(lax.axis_index("k") == 0, load_ref[:vectors], load_ref[vectors:])
    mine_ref[...] = load
    copies[2].wait()
    high, low = split(inverse_ref[...])
    high_ref[...] = high
    low_ref[...] = low
    y = jnp.where(in_level(row_code, 0, panels), solve(load, high_ref, low_ref, "nt"), 0.0)
    y_ref[...] = y
    send_to_all(send_ref, y)
    copies[3].wait()


def update_kernel(level, room, front_ref, partner_ref, got_ref, row_code_ref, col_code_ref, *refs):
    first, last = level == 1, level == LEVELS - 1
    got = got_ref[lax.axis_index("z")]
    if not first:
        got = place(got.astype(F32), col_code_ref[...], (level - 1) * 8, room).astype(BF16)
    half = front_ref.shape[1]
    left, right = got[:, :half], got[:, half:]
    on_left = lax.axis_index("k") == 0
    out = matmul(jnp.where(on_left, left, right), front_ref[...], "nt") + matmul(
        jnp.where(on_left, right, left), partner_ref[...], "nt"
    )
    if not first:
        out = refs[0][...] + out
    if not last:
        refs[-2][...] = out
    send_to_all(refs[-1], pick(out, row_code_ref[...], level * 8, room))


def forward_step(level, room, got_ref, mine_ref, code, high_ref, low_ref):
    return solve(mine_ref[...] - place(sum_slots(got_ref), code, level * 8, room), high_ref, low_ref, "nt")


def forward_kernel(level, room, got_ref, mine_ref, row_code_ref, high_ref, low_ref, y_in_ref, y_ref, send_ref):
    code = row_code_ref[...]
    candidate = forward_step(level, room, got_ref, mine_ref, code, high_ref, low_ref)
    y_ref[...] = jnp.where(in_level(code, level, 8), candidate, y_in_ref[...])
    send_to_all(send_ref, pick(candidate, code, level * 8, room))


def back_product(x, front_ref, partner_ref):
    x = x.astype(BF16)
    own, other = matmul(x, front_ref[...], "nn"), matmul(x, partner_ref[...], "nn")
    first = lax.axis_index("k") == 0
    return jnp.concatenate([jnp.where(first, own, other), jnp.where(first, other, own)], axis=1)


def turn_kernel(
    room, front_ref, partner_ref, got_ref, mine_ref, row_code_ref, col_code_ref, high_ref, low_ref, y_in_ref,
    modes_hbm, y_ref, x_ref, pending_ref, send_ref, modes_ref, sem,
):
    modes_copy = pltpu.make_async_copy(modes_hbm, modes_ref, sem)
    modes_copy.start()
    code = row_code_ref[...]
    level = LEVELS - 1
    chosen = in_level(code, level, 8)
    candidate = forward_step(level, room, got_ref, mine_ref, code, high_ref, low_ref)
    y = jnp.where(chosen, candidate, y_in_ref[...])
    y_ref[...] = y
    x = jnp.where(chosen, solve(y, high_ref, low_ref, "nn"), 0.0)
    x_ref[...] = x
    out = back_product(x, front_ref, partner_ref)
    pending_ref[...] = out
    send_to_all(send_ref, pick(out, col_code_ref[...], (level - 1) * 8, room))
    modes_copy.wait()


def back_kernel(level, room, got_ref, col_code_ref, high_ref, low_ref, y_ref, send_ref):
    code = col_code_ref[...]
    here = place(sum_slots(got_ref), code, level * 8, room)
    send_to_all(send_ref, pick(solve(y_ref[...] - here, high_ref, low_ref, "nn"), code, level * 8, room))


def fresh_rows(level, room, got_ref, row_code_ref):
    got = got_ref[lax.axis_index(PLANE)].astype(F32)
    return place(got, row_code_ref[...], level * 8, room)


def back_update_kernel(
    level, room, front_ref, partner_ref, got_ref, row_code_ref, col_code_ref, x_in_ref, pending_in_ref, x_ref, *refs
):
    fresh = fresh_rows(level, room, got_ref, row_code_ref)
    x_ref[...] = x_in_ref[...] + fresh
    out = pending_in_ref[...] + back_product(fresh, front_ref, partner_ref)
    if level > 1:
        refs[0][...] = out
    send_to_all(refs[-1], pick(out, col_code_ref[...], (level - 1) * 8, room))


def last_pick_kernel(room, got_ref, row_code_ref, x_in_ref, x_ref):
    x_ref[...] = x_in_ref[...] + fresh_rows(0, room, got_ref, row_code_ref)


def coords_kernel(pair_ref, tie_ref, mass_ref, modes_ref, x_ref, static_ref, send_ref):
    x = jnp.concatenate([pair_ref[0], pair_ref[1]], axis=0)
    x_ref[...] = x
    static = tie_ref[...] * x
    static_ref[...] = static
    coords = matmul((mass_ref[...] * static).astype(BF16), modes_ref[...], "nt").astype(BF16)
    cores, half = 2, send_ref.shape[2]
    for slot in range(send_ref.shape[0]):
        part = slot % cores
        send_ref[slot] = coords[:, part * half : (part + 1) * half]


def relay_kernel(got_ref, send_ref):
    send_to_all(send_ref, sum_slots(got_ref))


def gathered_kernel(got_ref, out_ref):
    out_ref[...] = sum_slots(got_ref).astype(BF16)


def finish_kernel(static_ref, pair_ref, modes_ref, x_ref, whole_ref, out_ref):
    half = pair_ref.shape[2]
    correction = matmul(pair_ref[0], modes_ref[:half], "nn") + matmul(pair_ref[1], modes_ref[half:], "nn")
    whole_ref[...] = x_ref[...]
    out_ref[:, 0, :] = static_ref[...] - correction


def bound(body, *settings):
    def kernel(*refs):
        return body(*settings, *refs)

    return kernel


def on_device(front, diag_inverse, load, panel_order, tie, mass, modes):
    vectors = load.shape[0]
    rows, half = front.shape
    plane = lax.axis_size(PLANE)
    depth = lax.axis_size("z")
    cores = lax.axis_size("k")
    mode_rows = modes.reshape(modes.shape[0], -1)

    part = vectors // cores
    panels, block = diag_inverse.shape[0], diag_inverse.shape[1]
    flat = ((part, rows), F32)
    coded = ((part, rows), jnp.int32)
    inverse_part = (diag_inverse.shape, BF16)
    narrow = ((vectors, half), BF16)
    to_depth = ((depth, vectors, half), BF16)

    def exchange(value, axes):
        return lax.all_to_all(value, axes, 0, 0, tiled=True)

    def both_cores(value):
        return lax.all_gather(value, "k", axis=0)

    row_code, col_code, high, low, mine, y, send, front = call(
        start_kernel,
        [coded, coded, inverse_part, inverse_part, flat, flat, ((plane, part, rows), BF16),
         (front.shape, BF16)],
        Far(panel_order[None, :]), Far(load), Far(diag_inverse), Far(front),
        scratch=[
            pltpu.VMEM((1, panel_order.shape[0]), jnp.int32),
            pltpu.VMEM(load.shape, F32),
            pltpu.VMEM(diag_inverse.shape, F32),
            pltpu.SemaphoreType.DMA((4,)),
        ],
    )

    got = exchange(send, PLANE)
    partner = lax.ppermute(front, "k", [(core, 1 - core) for core in range(cores)])

    def solve_levels(room, front, partner, got, row_code, col_code, high, low, mine, y, mode_rows):
        mode_shape = mode_rows.shape
        slots = ((plane, part, room * block), BF16)
        deep = ((depth, part, room * block), BF16)
        pending = ()
        for level in range(1, LEVELS):
            last = level == LEVELS - 1
            *pending, send = call(
                bound(update_kernel, level, room),
                [deep] if last else [flat, deep],
                front, partner, got, row_code, col_code, *pending,
            )
            got = exchange(send, "z")
            if not last:
                y, send = call(
                    bound(forward_kernel, level, room), [flat, slots], got, mine, row_code, high, low, y
                )
                got = exchange(send, PLANE)
        y, x, pending, send, mode_rows = call(
            bound(turn_kernel, room), [flat, flat, flat, slots, (mode_shape, BF16)],
            front, partner, got, mine, row_code, col_code, high, low, y, Far(mode_rows),
            scratch=[pltpu.SemaphoreType.DMA(())],
        )
        for level in reversed(range(LEVELS - 1)):
            (send,) = call(
                bound(back_kernel, level, room), [deep], exchange(send, PLANE), col_code, high, low, y
            )
            got = exchange(send, "z")
            if level > 0:
                x, *rest, send = call(
                    bound(back_update_kernel, level, room),
                    [flat, flat, slots] if level > 1 else [flat, slots],
                    front, partner, got, row_code, col_code, x, pending,
                )
                pending = rest[0] if rest else None
            else:
                (x,) = call(bound(last_pick_kernel, room), [flat], got, row_code, x)
        return x, mode_rows

    blocks = jnp.arange(plane, dtype=jnp.int32)
    inside = (panel_order.reshape(LEVELS, -1, 1) // panels) == blocks
    most = jnp.max(jnp.sum(inside.astype(jnp.int32), axis=1))
    rooms = ROOM + (panels,)
    choice = sum((most > room).astype(jnp.int32) for room in ROOM)
    x, mode_rows = lax.switch(
        choice,
        [bound(solve_levels, room) for room in rooms],
        front, partner, got, row_code, col_code, high, low, mine, y, mode_rows,
    )

    whole, static, send = call(
        coords_kernel,
        [((vectors, rows), F32), ((vectors, rows), F32), ((plane * cores, vectors, half), BF16)],
        both_cores(x), tie, mass, mode_rows,
    )
    (send,) = call(relay_kernel, [to_depth], exchange(send, PLANE + ("k",)))
    (coords,) = call(gathered_kernel, [narrow], exchange(send, "z"))
    return tuple(
        call(
            finish_kernel,
            [jax.ShapeDtypeStruct((vectors, rows), F32), jax.ShapeDtypeStruct((vectors, 1, rows), F32)],
            static, both_cores(coords), mode_rows, whole,
        )
    )


def solution(mesh):
    grid = Mesh(mesh.devices.reshape(4, 4, 16, 2), PLANE + ("z", "k"))
    row, col = PLANE, ("z", "k")
    in_specs = (
        P(row, col),
        P(row, None, None),
        P(None, row),
        P(),
        P(col, row),
        P(col, row),
        P(None, col, row),
    )
    out_specs = (P(None, row), P(None, col, row))
    return jax.shard_map(on_device, mesh=grid, in_specs=in_specs, out_specs=out_specs, check_vma=False)
```

time: 233 us -> 229 us (0.983)
  blocking collectives: 213 us -> 198 us
  starting transfers between devices: 8.75 us -> 12.3 us
  waiting for transfers between devices: 0.01 us -> 3.22 us
    all_to_all x14 -> x13, blocking collectives: 193 us -> 177 us  [exchange(): return lax.all_to_all(value, axes, 0, 0, tiled=True)]
    all_to_all x0 -> x1, starting transfers between devices: none -> 3.52 us  [exchange(): return lax.all_to_all(value, axes, 0, 0, tiled=True)]
    all_to_all x0 -> x1, waiting for transfers between devices: none -> 3.22 us  [exchange(): return lax.all_to_all(value, axes, 0, 0, tiled=True)]
  transfers between devices with their start and end apart: 1 -> 2, of which waited for: 0 -> 1; matrix products, arithmetic and copies ran while one was open for 0% -> 1% of each run, Pallas kernels for 1% -> 0%
where the time goes in v4:
time: 229 us; the launch traced here: 228 us
  blocking collectives  198 us (86%)
  starting transfers between devices  12.3 us (5%)
  Pallas kernels  10.2 us (4%)
  waiting for transfers between devices  3.22 us (1%)
  between operations  2.63 us (1%)
    all_to_all x13, blocking collectives, exchange(): return lax.all_to_all(value, axes, 0, 0, tiled=True)  177 us
    all_gather x2, blocking collectives, both_cores(): return lax.all_gather(value, 'k', axis=0)  20.3 us
    pallas_call x17, Pallas kernels, call(): pl.pallas_call(body, out_shape=[out if isinstance(out, jax.ShapeDtypeStru...  10.2 us
    ppermute x1, starting transfers between devices, on_device(): lax.ppermute(front, 'k', [(core, 1 - core) for core in range(cores)])  8.75 us
  transfers between devices with their start and end apart: 2, of which 1 were waited for; matrix products, arithmetic and copies ran while one was open for 1% of the time, Pallas kernels for 0%

profile of v4, /device:TPU:1, one launch (start us, length us, event | category | flops | bytes accessed | tf_op | source)
XLA Modules:
  0.0 227.9 jit_solution(156013142981272202)
XLA Ops:
  0.6 2.2 shard_map.86
  2.8 8.7 %collective-permute-start = (bf16[1024,512]{1,0:T(8,128)(2,1)S(1)}, bf16[1024,512]{1,0:T(8,128)(2,1)S(1)}, u32[]{:S(2)}, u32[]{:S(2)}) collective-permute-start(bf16[1024,512]{1,0:T(8,128)(2,1)S(1)} %get-tuple-element.207), channel_id=1, source_target_pairs={{0,1},{1,0},{2,3},{3,2},{4,5},{5,4},{6,7},{7,6},{8,9},{9,8},{10,11... | collective-permute-start | bytes 3145736 | tf_op jit(solution)/shard_map/ppermute | solution.py:307
  11.6 3.5 %all-to-all-start.44 = ((bf16[16,4,1024]{2,1,0:T(4,128)(2,1)}), bf16[16,4,1024]{2,1,0:T(4,128)(2,1)S(1)}, u32[]{:S(2)}, u32[]{:S(2)}) async-start(bf16[16,4,1024]{2,1,0:T(4,128)(2,1)} %get-tuple-element.208), calls=%async_computation.44 | async-start | bytes 262144 | tf_op jit(solution)/shard_map/all_to_all | solution.py:288
  15.1 0.7 reshape.69
  18.6 3.2 %all-to-all-done.44 = bf16[16,4,1024]{2,1,0:T(4,128)(2,1)S(1)} async-done(((bf16[16,4,1024]{2,1,0:T(4,128)(2,1)}), bf16[16,4,1024]{2,1,0:T(4,128)(2,1)S(1)}, u32[]{:S(2)}, u32[]{:S(2)}) %all-to-all-start.44) | async-done | bytes 131104 | tf_op jit(solution)/shard_map/all_to_all | solution.py:288
  21.8 156.2 %conditional.1 = (f32[4,1024]{1,0:T(4,128)S(1)}, bf16[1024,1024]{1,0:T(8,128)(2,1)S(1)}) conditional(s32[]{:T(128)} %clamp.3, (bf16[1024,512]{1,0:T(8,128)(2,1)S(1)}, bf16[1024,512]{1,0:T(8,128)(2,1)S(1)}, bf16[16,4,1024]{2,1,0:T(4,128)(2,1)S(1)}, s32[4,1024]{1,0:T(4,128)S(1)}, s32[4,1024]{1,0:T(4,128)S(1)}, ...), branch_computations={%region_2.3_spmd, %region_3.4_spmd, %region_4.5_spmd, %region_5.6_... | conditional | bytes 2883600 | solution.py:353
  22.7 24.5 %all_to_all.213.refs_0_ = bf16[16,4,768]{2,1,0:T(4,128)(2,1)S(1)} all-to-all(bf16[16,4,768]{2,1,0:T(4,128)(2,1)S(1)} %get-tuple-element.141), channel_id=1, replica_groups=mesh['x'=4,'y'=4,'z'=16,'k'=2] {'z'}, dimensions={0} | all-to-all | bytes 196608 | tf_op jit(solution)/shard_map/cond/branch_2_fun/all_to_all | solution.py:288
  47.6 10.0 %all_to_all.214.refs_2_ = bf16[16,4,768]{2,1,0:T(4,128)(2,1)S(1)} all-to-all(bf16[16,4,768]{2,1,0:T(4,128)(2,1)S(1)} %get-tuple-element.146), channel_id=1, replica_groups=mesh['x'=4,'y'=4,'z'=16,'k'=2] {'x','y'}, dimensions={0} | all-to-all | bytes 196608 | tf_op jit(solution)/shard_map/cond/branch_2_fun/all_to_all | solution.py:288
  58.2 16.2 %all_to_all.215.refs_0_ = bf16[16,4,768]{2,1,0:T(4,128)(2,1)S(1)} all-to-all(bf16[16,4,768]{2,1,0:T(4,128)(2,1)S(1)} %get-tuple-element.148), channel_id=1, replica_groups=mesh['x'=4,'y'=4,'z'=16,'k'=2] {'z'}, dimensions={0} | all-to-all | bytes 196608 | tf_op jit(solution)/shard_map/cond/branch_2_fun/all_to_all | solution.py:288
  74.8 9.9 %all_to_all.216.refs_2_ = bf16[16,4,768]{2,1,0:T(4,128)(2,1)S(1)} all-to-all(bf16[16,4,768]{2,1,0:T(4,128)(2,1)S(1)} %get-tuple-element.150), channel_id=1, replica_groups=mesh['x'=4,'y'=4,'z'=16,'k'=2] {'x','y'}, dimensions={0} | all-to-all | bytes 196608 | tf_op jit(solution)/shard_map/cond/branch_2_fun/all_to_all | solution.py:288
  84.8 0.7 branch_2_fun.16
  85.5 15.2 %all_to_all.217.refs_2_ = bf16[16,4,768]{2,1,0:T(4,128)(2,1)S(1)} all-to-all(bf16[16,4,768]{2,1,0:T(4,128)(2,1)S(1)} %branch_2_fun.16), channel_id=1, replica_groups=mesh['x'=4,'y'=4,'z'=16,'k'=2] {'z'}, dimensions={0} | all-to-all | bytes 196608 | tf_op jit(solution)/shard_map/cond/branch_2_fun/all_to_all | solution.py:288
  100.7 1.8 branch_2_fun.17
  102.5 9.6 %all_to_all.218.refs_0_ = bf16[16,4,768]{2,1,0:T(4,128)(2,1)S(1)} all-to-all(bf16[16,4,768]{2,1,0:T(4,128)(2,1)S(1)} %get-tuple-element.154), channel_id=1, replica_groups=mesh['x'=4,'y'=4,'z'=16,'k'=2] {'x','y'}, dimensions={0} | all-to-all | bytes 196608 | tf_op jit(solution)/shard_map/cond/branch_2_fun/all_to_all | solution.py:288
  112.4 15.0 %all_to_all.219.refs_2_ = bf16[16,4,768]{2,1,0:T(4,128)(2,1)S(1)} all-to-all(bf16[16,4,768]{2,1,0:T(4,128)(2,1)S(1)} %branch_2_fun.18), channel_id=1, replica_groups=mesh['x'=4,'y'=4,'z'=16,'k'=2] {'z'}, dimensions={0} | all-to-all | bytes 196608 | tf_op jit(solution)/shard_map/cond/branch_2_fun/all_to_all | solution.py:288
  127.8 9.6 %all_to_all.220.refs_0_ = bf16[16,4,768]{2,1,0:T(4,128)(2,1)S(1)} all-to-all(bf16[16,4,768]{2,1,0:T(4,128)(2,1)S(1)} %get-tuple-element.158), channel_id=1, replica_groups=mesh['x'=4,'y'=4,'z'=16,'k'=2] {'x','y'}, dimensions={0} | all-to-all | bytes 196608 | tf_op jit(solution)/shard_map/cond/branch_2_fun/all_to_all | solution.py:288
  137.7 14.8 %all_to_all.221.refs_2_ = bf16[16,4,768]{2,1,0:T(4,128)(2,1)S(1)} all-to-all(bf16[16,4,768]{2,1,0:T(4,128)(2,1)S(1)} %branch_2_fun.20), channel_id=1, replica_groups=mesh['x'=4,'y'=4,'z'=16,'k'=2] {'z'}, dimensions={0} | all-to-all | bytes 196608 | tf_op jit(solution)/shard_map/cond/branch_2_fun/all_to_all | solution.py:288
  153.0 9.9 %all_to_all.222.refs_0_ = bf16[16,4,768]{2,1,0:T(4,128)(2,1)S(1)} all-to-all(bf16[16,4,768]{2,1,0:T(4,128)(2,1)S(1)} %get-tuple-element.161), channel_id=1, replica_groups=mesh['x'=4,'y'=4,'z'=16,'k'=2] {'x','y'}, dimensions={0} | all-to-all | bytes 196608 | tf_op jit(solution)/shard_map/cond/branch_2_fun/all_to_all | solution.py:288
  163.2 14.8 %all_to_all.223.refs_0_ = bf16[16,4,768]{2,1,0:T(4,128)(2,1)S(1)} all-to-all(bf16[16,4,768]{2,1,0:T(4,128)(2,1)S(1)} %branch_2_fun.22), channel_id=1, replica_groups=mesh['x'=4,'y'=4,'z'=16,'k'=2] {'z'}, dimensions={0} | all-to-all | bytes 196608 | tf_op jit(solution)/shard_map/cond/branch_2_fun/all_to_all | solution.py:288
  178.0 16.0 %all-gather.2.pair_ref = f32[2,4,1024]{2,1,0:T(4,128)S(1)} all-gather(f32[1,4,1024]{2,1,0:T(4,128)S(1)} %bitcast.5), channel_id=2, replica_groups=mesh['x'=4,'y'=4,'z'=16,'k'=2] {'k'}, dimensions={0}, use_global_device_ids=true | all-gather | bytes 49152 | tf_op jit(solution)/shard_map/all_gather | solution.py:291
  194.7 12.7 %all_to_all.235.got_ref = bf16[32,8,512]{2,1,0:T(8,128)(2,1)S(1)} all-to-all(bf16[32,8,512]{2,1,0:T(8,128)(2,1)S(1)} %get-tuple-element.218), channel_id=1, replica_groups=mesh['x'=4,'y'=4,'z'=16,'k'=2] {'x','y','k'}, dimensions={0} | all-to-all | bytes 524288 | tf_op jit(solution)/shard_map/all_to_all | solution.py:288
  207.5 15.0 %all_to_all.236.got_ref = bf16[16,8,512]{2,1,0:T(8,128)(2,1)S(1)} all-to-all(bf16[16,8,512]{2,1,0:T(8,128)(2,1)S(1)} %shard_map.88), channel_id=1, replica_groups=mesh['x'=4,'y'=4,'z'=16,'k'=2] {'z'}, dimensions={0} | all-to-all | bytes 262144 | tf_op jit(solution)/shard_map/all_to_all | solution.py:288
  222.5 4.3 %all-gather.1 = bf16[16,512]{1,0:T(8,128)(2,1)S(1)} all-gather(bf16[8,512]{1,0:T(8,128)(2,1)S(1)} %shard_map.89), channel_id=3, replica_groups=mesh['x'=4,'y'=4,'z'=16,'k'=2] {'k'}, dimensions={0}, use_global_device_ids=true | all-gather | bytes 24576 | tf_op jit(solution)/shard_map/all_gather | solution.py:291
  226.8 1.0 shard_map.90
  (21 shorter events, 5.4 us)
Async XLA Ops:
  2.8 19.0 %collective-permute-start = (bf16[1024,512]{1,0:T(8,128)(2,1)S(1)}, bf16[1024,512]{1,0:T(8,128)(2,1)S(1)}, u32[]{:S(2)}, u32[]{:S(2)}) collective-permute-start(bf16[1024,512]{1,0:T(8,128)(2,1)S(1)} %get-tuple-element.207), channel_id=1, source_target_pairs={{0,1},{1,0},{2,3},{3,2},{4,5},{5,4},{6,7},{7,6},{8,9},{9,8},{10,11... | collective-permute-start | bytes 3145736 | tf_op jit(solution)/shard_map/ppermute | solution.py:307
  11.6 10.2 %all-to-all-start.44 = ((bf16[16,4,1024]{2,1,0:T(4,128)(2,1)}), bf16[16,4,1024]{2,1,0:T(4,128)(2,1)S(1)}, u32[]{:S(2)}, u32[]{:S(2)}) async-start(bf16[16,4,1024]{2,1,0:T(4,128)(2,1)} %get-tuple-element.208), calls=%async_computation.44 | async-start | bytes 262144 | tf_op jit(solution)/shard_map/all_to_all | solution.py:288
  21.8 172.2 %copy-start = (f32[1,1024]{1,0:T(1,128)S(1)}, f32[1,1024]{1,0:T(1,128)}, u32[]{:S(2)}) copy-start(f32[1,1024]{1,0:T(1,128)} %tie_ref.1) | copy-start | bytes 12292
  21.8 172.2 %copy-start.1 = (f32[1,1024]{1,0:T(1,128)S(1)}, f32[1,1024]{1,0:T(1,128)}, u32[]{:S(2)}) copy-start(f32[1,1024]{1,0:T(1,128)} %mass_ref.1) | copy-start | bytes 12292

commit v5 on v4

--- a/solution.py
+++ b/solution.py
@@ -20,6 +20,9 @@
 def split(value):
     high = value.astype(BF16)
     return high, (value - high.astype(F32)).astype(BF16)
+
+
+CHOICE = pltpu.SMEM((1,), jnp.int32)
 
 
 class Far:
@@ -39,9 +42,9 @@
             given.append(pltpu.with_memory_space_constraint(arg, pltpu.VMEM))
     return pl.pallas_call(
         body,
-        out_shape=[out if isinstance(out, jax.ShapeDtypeStruct) else pltpu.VMEM(*out) for out in outs],
+        out_shape=[pltpu.VMEM(*out) if isinstance(out, tuple) else out for out in outs],
         in_specs=in_specs,
-        out_specs=[vmem] * len(outs),
+        out_specs=[pl.BlockSpec(memory_space=pltpu.SMEM) if out is CHOICE else vmem for out in outs],
         scratch_shapes=list(scratch),
         compiler_params=pltpu.CompilerParams(vmem_limit_bytes=8 << 20),
     )(*given)
@@ -105,7 +108,7 @@
 
 def start_kernel(
     order_hbm, load_hbm, inverse_hbm, front_hbm,
-    row_code_ref, col_code_ref, high_ref, low_ref, mine_ref, y_ref, send_ref, front_ref,
+    row_code_ref, col_code_ref, high_ref, low_ref, mine_ref, y_ref, send_ref, front_ref, choice_ref,
     order_ref, load_ref, inverse_ref, sems,
 ):
     panels, block = high_ref.shape[0], high_ref.shape[1]
@@ -139,6 +142,15 @@
     row_code = jnp.concatenate(spread_codes[:panels], axis=1)
     row_code_ref[...] = row_code
     col_code_ref[...] = jnp.concatenate(spread_codes[panels:], axis=1)
+    inside = order // panels == panel
+    most = jnp.zeros((2 * panels, 1), jnp.int32)
+    for level in range(LEVELS):
+        of_level = inside & (counting >= level * per_level) & (counting < (level + 1) * per_level)
+        most = jnp.maximum(most, jnp.sum(jnp.where(of_level, 1, 0), axis=1, keepdims=True))
+    choice = jnp.zeros_like(most)
+    for room in ROOM:
+        choice = choice + jnp.where(most > room, 1, 0)
+    choice_ref[0] = jnp.max(choice)
     copies[1].wait()
     load = jnp.where(lax.axis_index("k") == 0, load_ref[:vectors], load_ref[vectors:])
     mine_ref[...] = load
@@ -290,10 +302,10 @@
     def both_cores(value):
         return lax.all_gather(value, "k", axis=0)
 
-    row_code, col_code, high, low, mine, y, send, front = call(
+    row_code, col_code, high, low, mine, y, send, front, choice = call(
         start_kernel,
         [coded, coded, inverse_part, inverse_part, flat, flat, ((plane, part, rows), BF16),
-         (front.shape, BF16)],
+         (front.shape, BF16), CHOICE],
         Far(panel_order[None, :]), Far(load), Far(diag_inverse), Far(front),
         scratch=[
             pltpu.VMEM((1, panel_order.shape[0]), jnp.int32),
@@ -345,13 +357,9 @@
                 (x,) = call(bound(last_pick_kernel, room), [flat], got, row_code, x)
         return x, mode_rows
 
-    blocks = jnp.arange(plane, dtype=jnp.int32)
-    inside = (panel_order.reshape(LEVELS, -1, 1) // panels) == blocks
-    most = jnp.max(jnp.sum(inside.astype(jnp.int32), axis=1))
     rooms = ROOM + (panels,)
-    choice = sum((most > room).astype(jnp.int32) for room in ROOM)
     x, mode_rows = lax.switch(
-        choice,
+        choice[0],
         [bound(solve_levels, room) for room in rooms],
         front, partner, got, row_code, col_code, high, low, mine, y, mode_rows,
     )

time: 229 us -> 229 us (level)
  waiting for transfers between devices: 3.22 us -> 6.71 us
    all_to_all x1, waiting for transfers between devices: 3.22 us -> 6.71 us  [exchange(): return lax.all_to_all(value, axes, 0, 0, tiled=True)]
  transfers between devices with their start and end apart: 2 -> 2, of which waited for: 1 -> 1; matrix products, arithmetic and copies ran while one was open for 1% -> 0% of each run, Pallas kernels for 0% -> 0%
where the time goes in v5:
time: 229 us; the launch traced here: 228 us
  blocking collectives  198 us (86%)
  starting transfers between devices  12.3 us (5%)
  Pallas kernels  10.2 us (4%)
  waiting for transfers between devices  6.71 us (3%)
    all_to_all x13, blocking collectives, exchange(): return lax.all_to_all(value, axes, 0, 0, tiled=True)  177 us
    all_gather x2, blocking collectives, both_cores(): return lax.all_gather(value, 'k', axis=0)  20.3 us
    pallas_call x17, Pallas kernels, call(): pl.pallas_call(body, out_shape=[pltpu.VMEM(*out) if isinstance(out, tuple...  10.2 us
    ppermute x1, starting transfers between devices, on_device(): lax.ppermute(front, 'k', [(core, 1 - core) for core in range(cores)])  8.75 us
    all_to_all x1, waiting for transfers between devices, exchange(): return lax.all_to_all(value, axes, 0, 0, tiled=True)  6.71 us
  transfers between devices with their start and end apart: 2, of which 1 were waited for; matrix products, arithmetic and copies ran while one was open for 0% of the time, Pallas kernels for 0%

profile of v5, /device:TPU:1, one launch (start us, length us, event | category | flops | bytes accessed | tf_op | source)
XLA Modules:
  0.0 227.8 jit_solution(3860025465817165732)
XLA Ops:
  0.6 2.2 shard_map.86
  2.8 8.7 %collective-permute-start = (bf16[1024,512]{1,0:T(8,128)(2,1)S(1)}, bf16[1024,512]{1,0:T(8,128)(2,1)S(1)}, u32[]{:S(2)}, u32[]{:S(2)}) collective-permute-start(bf16[1024,512]{1,0:T(8,128)(2,1)S(1)} %get-tuple-element.209), channel_id=1, source_target_pairs={{0,1},{1,0},{2,3},{3,2},{4,5},{5,4},{6,7},{7,6},{8,9},{9,8},{10,11... | collective-permute-start | bytes 3145736 | tf_op jit(solution)/shard_map/ppermute | solution.py:319
  11.6 3.5 %all-to-all-start.44 = ((bf16[16,4,1024]{2,1,0:T(4,128)(2,1)}), bf16[16,4,1024]{2,1,0:T(4,128)(2,1)S(1)}, u32[]{:S(2)}, u32[]{:S(2)}) async-start(bf16[16,4,1024]{2,1,0:T(4,128)(2,1)} %get-tuple-element.210), calls=%async_computation.44 | async-start | bytes 262144 | tf_op jit(solution)/shard_map/all_to_all | solution.py:300
  15.1 6.7 %all-to-all-done.44 = bf16[16,4,1024]{2,1,0:T(4,128)(2,1)S(1)} async-done(((bf16[16,4,1024]{2,1,0:T(4,128)(2,1)}), bf16[16,4,1024]{2,1,0:T(4,128)(2,1)S(1)}, u32[]{:S(2)}, u32[]{:S(2)}) %all-to-all-start.44) | async-done | bytes 131104 | tf_op jit(solution)/shard_map/all_to_all | solution.py:300
  21.8 156.2 %conditional.1 = (f32[4,1024]{1,0:T(4,128)S(1)}, bf16[1024,1024]{1,0:T(8,128)(2,1)S(1)}) conditional(s32[]{:T(128)} %bitcast.1, (bf16[1024,512]{1,0:T(8,128)(2,1)S(1)}, bf16[1024,512]{1,0:T(8,128)(2,1)S(1)}, bf16[16,4,1024]{2,1,0:T(4,128)(2,1)S(1)}, s32[4,1024]{1,0:T(4,128)S(1)}, s32[4,1024]{1,0:T(4,128)S(1)}, ...), branch_computations={%region_0.0_spmd, %region_1.0_spmd, %region_2.0_spmd, %region_3.0_... | conditional | bytes 2883600 | solution.py:361
  22.7 24.5 %all_to_all.213.refs_0_ = bf16[16,4,768]{2,1,0:T(4,128)(2,1)S(1)} all-to-all(bf16[16,4,768]{2,1,0:T(4,128)(2,1)S(1)} %get-tuple-element.141), channel_id=1, replica_groups=mesh['x'=4,'y'=4,'z'=16,'k'=2] {'z'}, dimensions={0} | all-to-all | bytes 196608 | tf_op jit(solution)/shard_map/cond/branch_2_fun/all_to_all | solution.py:300
  47.6 10.0 %all_to_all.214.refs_2_ = bf16[16,4,768]{2,1,0:T(4,128)(2,1)S(1)} all-to-all(bf16[16,4,768]{2,1,0:T(4,128)(2,1)S(1)} %get-tuple-element.146), channel_id=1, replica_groups=mesh['x'=4,'y'=4,'z'=16,'k'=2] {'x','y'}, dimensions={0} | all-to-all | bytes 196608 | tf_op jit(solution)/shard_map/cond/branch_2_fun/all_to_all | solution.py:300
  57.5 0.7 branch_2_fun.14
  58.2 16.2 %all_to_all.215.refs_0_ = bf16[16,4,768]{2,1,0:T(4,128)(2,1)S(1)} all-to-all(bf16[16,4,768]{2,1,0:T(4,128)(2,1)S(1)} %get-tuple-element.148), channel_id=1, replica_groups=mesh['x'=4,'y'=4,'z'=16,'k'=2] {'z'}, dimensions={0} | all-to-all | bytes 196608 | tf_op jit(solution)/shard_map/cond/branch_2_fun/all_to_all | solution.py:300
  74.8 9.9 %all_to_all.216.refs_2_ = bf16[16,4,768]{2,1,0:T(4,128)(2,1)S(1)} all-to-all(bf16[16,4,768]{2,1,0:T(4,128)(2,1)S(1)} %get-tuple-element.150), channel_id=1, replica_groups=mesh['x'=4,'y'=4,'z'=16,'k'=2] {'x','y'}, dimensions={0} | all-to-all | bytes 196608 | tf_op jit(solution)/shard_map/cond/branch_2_fun/all_to_all | solution.py:300
  84.8 0.7 branch_2_fun.16
  85.4 15.2 %all_to_all.217.refs_2_ = bf16[16,4,768]{2,1,0:T(4,128)(2,1)S(1)} all-to-all(bf16[16,4,768]{2,1,0:T(4,128)(2,1)S(1)} %branch_2_fun.16), channel_id=1, replica_groups=mesh['x'=4,'y'=4,'z'=16,'k'=2] {'z'}, dimensions={0} | all-to-all | bytes 196608 | tf_op jit(solution)/shard_map/cond/branch_2_fun/all_to_all | solution.py:300
  100.6 1.8 branch_2_fun.17
  102.5 9.6 %all_to_all.218.refs_0_ = bf16[16,4,768]{2,1,0:T(4,128)(2,1)S(1)} all-to-all(bf16[16,4,768]{2,1,0:T(4,128)(2,1)S(1)} %get-tuple-element.154), channel_id=1, replica_groups=mesh['x'=4,'y'=4,'z'=16,'k'=2] {'x','y'}, dimensions={0} | all-to-all | bytes 196608 | tf_op jit(solution)/shard_map/cond/branch_2_fun/all_to_all | solution.py:300
  112.4 15.0 %all_to_all.219.refs_2_ = bf16[16,4,768]{2,1,0:T(4,128)(2,1)S(1)} all-to-all(bf16[16,4,768]{2,1,0:T(4,128)(2,1)S(1)} %branch_2_fun.18), channel_id=1, replica_groups=mesh['x'=4,'y'=4,'z'=16,'k'=2] {'z'}, dimensions={0} | all-to-all | bytes 196608 | tf_op jit(solution)/shard_map/cond/branch_2_fun/all_to_all | solution.py:300
  127.8 9.6 %all_to_all.220.refs_0_ = bf16[16,4,768]{2,1,0:T(4,128)(2,1)S(1)} all-to-all(bf16[16,4,768]{2,1,0:T(4,128)(2,1)S(1)} %get-tuple-element.158), channel_id=1, replica_groups=mesh['x'=4,'y'=4,'z'=16,'k'=2] {'x','y'}, dimensions={0} | all-to-all | bytes 196608 | tf_op jit(solution)/shard_map/cond/branch_2_fun/all_to_all | solution.py:300
  137.7 14.8 %all_to_all.221.refs_2_ = bf16[16,4,768]{2,1,0:T(4,128)(2,1)S(1)} all-to-all(bf16[16,4,768]{2,1,0:T(4,128)(2,1)S(1)} %branch_2_fun.20), channel_id=1, replica_groups=mesh['x'=4,'y'=4,'z'=16,'k'=2] {'z'}, dimensions={0} | all-to-all | bytes 196608 | tf_op jit(solution)/shard_map/cond/branch_2_fun/all_to_all | solution.py:300
  153.0 9.9 %all_to_all.222.refs_0_ = bf16[16,4,768]{2,1,0:T(4,128)(2,1)S(1)} all-to-all(bf16[16,4,768]{2,1,0:T(4,128)(2,1)S(1)} %get-tuple-element.161), channel_id=1, replica_groups=mesh['x'=4,'y'=4,'z'=16,'k'=2] {'x','y'}, dimensions={0} | all-to-all | bytes 196608 | tf_op jit(solution)/shard_map/cond/branch_2_fun/all_to_all | solution.py:300
  163.2 14.8 %all_to_all.223.refs_0_ = bf16[16,4,768]{2,1,0:T(4,128)(2,1)S(1)} all-to-all(bf16[16,4,768]{2,1,0:T(4,128)(2,1)S(1)} %branch_2_fun.22), channel_id=1, replica_groups=mesh['x'=4,'y'=4,'z'=16,'k'=2] {'z'}, dimensions={0} | all-to-all | bytes 196608 | tf_op jit(solution)/shard_map/cond/branch_2_fun/all_to_all | solution.py:300
  178.0 16.0 %all-gather.2.pair_ref = f32[2,4,1024]{2,1,0:T(4,128)S(1)} all-gather(f32[1,4,1024]{2,1,0:T(4,128)S(1)} %bitcast.6), channel_id=2, replica_groups=mesh['x'=4,'y'=4,'z'=16,'k'=2] {'k'}, dimensions={0}, use_global_device_ids=true | all-gather | bytes 49152 | tf_op jit(solution)/shard_map/all_gather | solution.py:303
  194.7 12.7 %all_to_all.235.got_ref = bf16[32,8,512]{2,1,0:T(8,128)(2,1)S(1)} all-to-all(bf16[32,8,512]{2,1,0:T(8,128)(2,1)S(1)} %get-tuple-element.220), channel_id=1, replica_groups=mesh['x'=4,'y'=4,'z'=16,'k'=2] {'x','y','k'}, dimensions={0} | all-to-all | bytes 524288 | tf_op jit(solution)/shard_map/all_to_all | solution.py:300
  207.5 15.0 %all_to_all.236.got_ref = bf16[16,8,512]{2,1,0:T(8,128)(2,1)S(1)} all-to-all(bf16[16,8,512]{2,1,0:T(8,128)(2,1)S(1)} %shard_map.88), channel_id=1, replica_groups=mesh['x'=4,'y'=4,'z'=16,'k'=2] {'z'}, dimensions={0} | all-to-all | bytes 262144 | tf_op jit(solution)/shard_map/all_to_all | solution.py:300
  222.5 4.3 %all-gather.1 = bf16[16,512]{1,0:T(8,128)(2,1)S(1)} all-gather(bf16[8,512]{1,0:T(8,128)(2,1)S(1)} %shard_map.89), channel_id=3, replica_groups=mesh['x'=4,'y'=4,'z'=16,'k'=2] {'k'}, dimensions={0}, use_global_device_ids=true | all-gather | bytes 24576 | tf_op jit(solution)/shard_map/all_gather | solution.py:303
  226.8 1.0 shard_map.90
  (17 shorter events, 3.9 us)
Async XLA Ops:
  2.8 19.0 %collective-permute-start = (bf16[1024,512]{1,0:T(8,128)(2,1)S(1)}, bf16[1024,512]{1,0:T(8,128)(2,1)S(1)}, u32[]{:S(2)}, u32[]{:S(2)}) collective-permute-start(bf16[1024,512]{1,0:T(8,128)(2,1)S(1)} %get-tuple-element.209), channel_id=1, source_target_pairs={{0,1},{1,0},{2,3},{3,2},{4,5},{5,4},{6,7},{7,6},{8,9},{9,8},{10,11... | collective-permute-start | bytes 3145736 | tf_op jit(solution)/shard_map/ppermute | solution.py:319
  11.6 10.2 %all-to-all-start.44 = ((bf16[16,4,1024]{2,1,0:T(4,128)(2,1)}), bf16[16,4,1024]{2,1,0:T(4,128)(2,1)S(1)}, u32[]{:S(2)}, u32[]{:S(2)}) async-start(bf16[16,4,1024]{2,1,0:T(4,128)(2,1)} %get-tuple-element.210), calls=%async_computation.44 | async-start | bytes 262144 | tf_op jit(solution)/shard_map/all_to_all | solution.py:300
  21.8 172.2 %copy-start = (f32[1,1024]{1,0:T(1,128)S(1)}, f32[1,1024]{1,0:T(1,128)}, u32[]{:S(2)}) copy-start(f32[1,1024]{1,0:T(1,128)} %tie_ref.1) | copy-start | bytes 12292
  21.8 172.2 %copy-start.1 = (f32[1,1024]{1,0:T(1,128)S(1)}, f32[1,1024]{1,0:T(1,128)}, u32[]{:S(2)}) copy-start(f32[1,1024]{1,0:T(1,128)} %mass_ref.1) | copy-start | bytes 12292

commit v6 on v5

--- a/solution.py
+++ b/solution.py
@@ -4,7 +4,6 @@
 from jax.experimental import pallas as pl
 from jax.experimental.pallas import tpu as pltpu
 from jax.sharding import Mesh, PartitionSpec as P
-
 
 LEVELS = 4
 ROOM = (4, 5, 6)
@@ -302,6 +301,7 @@
     def both_cores(value):
         return lax.all_gather(value, "k", axis=0)
 
+    partner = lax.ppermute(front, "k", [(core, 1 - core) for core in range(cores)])
     row_code, col_code, high, low, mine, y, send, front, choice = call(
         start_kernel,
         [coded, coded, inverse_part, inverse_part, flat, flat, ((plane, part, rows), BF16),
@@ -315,8 +315,7 @@
         ],
     )
 
-    got = exchange(send, PLANE)
-    partner = lax.ppermute(front, "k", [(core, 1 - core) for core in range(cores)])
+    got, choice = lax.optimization_barrier((exchange(send, PLANE), choice))
 
     def solve_levels(room, front, partner, got, row_code, col_code, high, low, mine, y, mode_rows):
         mode_shape = mode_rows.shape
@@ -393,4 +392,6 @@
         P(None, col, row),
     )
     out_specs = (P(None, row), P(None, col, row))
-    return jax.shard_map(on_device, mesh=grid, in_specs=in_specs, out_specs=out_specs, check_vma=False)
+    return jax.shard_map(
+        on_device, mesh=grid, in_specs=in_specs, out_specs=out_specs, check_vma=False
+    )

time: 229 us -> 223 us (0.974)
  waiting for transfers between devices: 6.71 us -> 0.01 us
  blocking collectives: 198 us -> 202 us
  starting transfers between devices: 12.3 us -> 8.75 us
    all_to_all x1 -> x0, waiting for transfers between devices: 6.71 us -> none  [exchange(): return lax.all_to_all(value, axes, 0, 0, tiled=True)]
    all_to_all x13 -> x14, blocking collectives: 177 us -> 181 us  [exchange(): return lax.all_to_all(value, axes, 0, 0, tiled=True)]
    all_to_all x1 -> x0, starting transfers between devices: 3.52 us -> none  [exchange(): return lax.all_to_all(value, axes, 0, 0, tiled=True)]
  transfers between devices with their start and end apart: 2 -> 1, of which waited for: 1 -> 0; matrix products, arithmetic and copies ran while one was open for 0% -> 0% of each run, Pallas kernels for 0% -> 1%
where the time goes in v6:
time: 223 us; the launch traced here: 221 us
  blocking collectives  202 us (91%)
  Pallas kernels  9.3 us (4%)
  starting transfers between devices  8.75 us (4%)
    all_to_all x14, blocking collectives, exchange(): return lax.all_to_all(value, axes, 0, 0, tiled=True)  181 us
    all_gather x2, blocking collectives, both_cores(): return lax.all_gather(value, 'k', axis=0)  20.7 us
    pallas_call x17, Pallas kernels, call(): pl.pallas_call(body, out_shape=[pltpu.VMEM(*out) if isinstance(out, tuple...  9.3 us
    ppermute x1, starting transfers between devices, on_device(): lax.ppermute(front, 'k', [(core, 1 - core) for core in range(cores)])  8.75 us
  transfers between devices with their start and end apart: 1, of which 0 were waited for; matrix products, arithmetic and copies ran while one was open for 0% of the time, Pallas kernels for 1%

profile of v6, /device:TPU:1, one launch (start us, length us, event | category | flops | bytes accessed | tf_op | source)
XLA Modules:
  0.0 220.9 jit_solution(14910449608810359334)
XLA Ops:
  0.6 8.7 %collective-permute-start = (bf16[1024,512]{1,0:T(8,128)(2,1)}, bf16[1024,512]{1,0:T(8,128)(2,1)S(1)}, u32[]{:S(2)}, u32[]{:S(2)}) collective-permute-start(bf16[1024,512]{1,0:T(8,128)(2,1)} %front_hbm.1), channel_id=1, source_target_pairs={{0,1},{1,0},{2,3},{3,2},{4,5},{5,4},{6,7},{7,6},{8,9},{9,8},{10,11... | collective-permute-start | bytes 3145736 | tf_op jit(solution)/shard_map/ppermute | solution.py:304
  9.4 1.5 shard_map.86
  10.9 9.3 %all_to_all.235 = bf16[16,4,1024]{2,1,0:T(4,128)(2,1)S(1)} all-to-all(bf16[16,4,1024]{2,1,0:T(4,128)(2,1)S(1)} %get-tuple-element.210), channel_id=1, replica_groups=mesh['x'=4,'y'=4,'z'=16,'k'=2] {'x','y'}, dimensions={0} | all-to-all | bytes 262144 | tf_op jit(solution)/shard_map/all_to_all | solution.py:299
  20.3 151.1 %conditional.1 = (f32[4,1024]{1,0:T(4,128)S(1)}, bf16[1024,1024]{1,0:T(8,128)(2,1)S(1)}) conditional(s32[]{:T(128)} %bitcast.1, (bf16[1024,512]{1,0:T(8,128)(2,1)S(1)}, bf16[1024,512]{1,0:T(8,128)(2,1)S(1)}, bf16[16,4,1024]{2,1,0:T(4,128)(2,1)S(1)}, s32[4,1024]{1,0:T(4,128)S(1)}, s32[4,1024]{1,0:T(4,128)S(1)}, ...), branch_computations={%region_0.0_spmd, %region_1.0_spmd, %region_2.0_spmd, %region_3.0_... | conditional | bytes 2883600 | solution.py:360
  20.3 0.7 branch_0_fun.12
  20.9 24.9 %all_to_all.191.refs_0_ = bf16[16,4,512]{2,1,0:T(4,128)(2,1)S(1)} all-to-all(bf16[16,4,512]{2,1,0:T(4,128)(2,1)S(1)} %get-tuple-element.85), channel_id=1, replica_groups=mesh['x'=4,'y'=4,'z'=16,'k'=2] {'z'}, dimensions={0} | all-to-all | bytes 131072 | tf_op jit(solution)/shard_map/cond/branch_0_fun/all_to_all | solution.py:299
  46.2 9.9 %all_to_all.192.refs_2_ = bf16[16,4,512]{2,1,0:T(4,128)(2,1)S(1)} all-to-all(bf16[16,4,512]{2,1,0:T(4,128)(2,1)S(1)} %get-tuple-element.90), channel_id=1, replica_groups=mesh['x'=4,'y'=4,'z'=16,'k'=2] {'x','y'}, dimensions={0} | all-to-all | bytes 131072 | tf_op jit(solution)/shard_map/cond/branch_0_fun/all_to_all | solution.py:299
  56.1 0.7 branch_0_fun.14
  56.8 14.4 %all_to_all.193.refs_0_ = bf16[16,4,512]{2,1,0:T(4,128)(2,1)S(1)} all-to-all(bf16[16,4,512]{2,1,0:T(4,128)(2,1)S(1)} %get-tuple-element.92), channel_id=1, replica_groups=mesh['x'=4,'y'=4,'z'=16,'k'=2] {'z'}, dimensions={0} | all-to-all | bytes 131072 | tf_op jit(solution)/shard_map/cond/branch_0_fun/all_to_all | solution.py:299
  71.6 9.5 %all_to_all.194.refs_2_ = bf16[16,4,512]{2,1,0:T(4,128)(2,1)S(1)} all-to-all(bf16[16,4,512]{2,1,0:T(4,128)(2,1)S(1)} %get-tuple-element.94), channel_id=1, replica_groups=mesh['x'=4,'y'=4,'z'=16,'k'=2] {'x','y'}, dimensions={0} | all-to-all | bytes 131072 | tf_op jit(solution)/shard_map/cond/branch_0_fun/all_to_all | solution.py:299
  81.7 14.4 %all_to_all.195.refs_2_ = bf16[16,4,512]{2,1,0:T(4,128)(2,1)S(1)} all-to-all(bf16[16,4,512]{2,1,0:T(4,128)(2,1)S(1)} %branch_0_fun.16), channel_id=1, replica_groups=mesh['x'=4,'y'=4,'z'=16,'k'=2] {'z'}, dimensions={0} | all-to-all | bytes 131072 | tf_op jit(solution)/shard_map/cond/branch_0_fun/all_to_all | solution.py:299
  96.1 1.6 branch_0_fun.17
  97.7 9.5 %all_to_all.196.refs_0_ = bf16[16,4,512]{2,1,0:T(4,128)(2,1)S(1)} all-to-all(bf16[16,4,512]{2,1,0:T(4,128)(2,1)S(1)} %get-tuple-element.98), channel_id=1, replica_groups=mesh['x'=4,'y'=4,'z'=16,'k'=2] {'x','y'}, dimensions={0} | all-to-all | bytes 131072 | tf_op jit(solution)/shard_map/cond/branch_0_fun/all_to_all | solution.py:299
  107.5 14.2 %all_to_all.197.refs_2_ = bf16[16,4,512]{2,1,0:T(4,128)(2,1)S(1)} all-to-all(bf16[16,4,512]{2,1,0:T(4,128)(2,1)S(1)} %branch_0_fun.18), channel_id=1, replica_groups=mesh['x'=4,'y'=4,'z'=16,'k'=2] {'z'}, dimensions={0} | all-to-all | bytes 131072 | tf_op jit(solution)/shard_map/cond/branch_0_fun/all_to_all | solution.py:299
  122.1 9.8 %all_to_all.198.refs_0_ = bf16[16,4,512]{2,1,0:T(4,128)(2,1)S(1)} all-to-all(bf16[16,4,512]{2,1,0:T(4,128)(2,1)S(1)} %get-tuple-element.102), channel_id=1, replica_groups=mesh['x'=4,'y'=4,'z'=16,'k'=2] {'x','y'}, dimensions={0} | all-to-all | bytes 131072 | tf_op jit(solution)/shard_map/cond/branch_0_fun/all_to_all | solution.py:299
  132.1 14.2 %all_to_all.199.refs_2_ = bf16[16,4,512]{2,1,0:T(4,128)(2,1)S(1)} all-to-all(bf16[16,4,512]{2,1,0:T(4,128)(2,1)S(1)} %branch_0_fun.20), channel_id=1, replica_groups=mesh['x'=4,'y'=4,'z'=16,'k'=2] {'z'}, dimensions={0} | all-to-all | bytes 131072 | tf_op jit(solution)/shard_map/cond/branch_0_fun/all_to_all | solution.py:299
  146.8 9.8 %all_to_all.200.refs_0_ = bf16[16,4,512]{2,1,0:T(4,128)(2,1)S(1)} all-to-all(bf16[16,4,512]{2,1,0:T(4,128)(2,1)S(1)} %get-tuple-element.105), channel_id=1, replica_groups=mesh['x'=4,'y'=4,'z'=16,'k'=2] {'x','y'}, dimensions={0} | all-to-all | bytes 131072 | tf_op jit(solution)/shard_map/cond/branch_0_fun/all_to_all | solution.py:299
  156.8 14.2 %all_to_all.201.refs_0_ = bf16[16,4,512]{2,1,0:T(4,128)(2,1)S(1)} all-to-all(bf16[16,4,512]{2,1,0:T(4,128)(2,1)S(1)} %branch_0_fun.22), channel_id=1, replica_groups=mesh['x'=4,'y'=4,'z'=16,'k'=2] {'z'}, dimensions={0} | all-to-all | bytes 131072 | tf_op jit(solution)/shard_map/cond/branch_0_fun/all_to_all | solution.py:299
  171.3 16.9 %all-gather.2.pair_ref = f32[2,4,1024]{2,1,0:T(4,128)S(1)} all-gather(f32[1,4,1024]{2,1,0:T(4,128)S(1)} %bitcast.6), channel_id=2, replica_groups=mesh['x'=4,'y'=4,'z'=16,'k'=2] {'k'}, dimensions={0}, use_global_device_ids=true | all-gather | bytes 49152 | tf_op jit(solution)/shard_map/all_gather | solution.py:302
  188.2 0.7 shard_map.87
  188.9 12.6 %all_to_all.236.got_ref = bf16[32,8,512]{2,1,0:T(8,128)(2,1)S(1)} all-to-all(bf16[32,8,512]{2,1,0:T(8,128)(2,1)S(1)} %get-tuple-element.224), channel_id=1, replica_groups=mesh['x'=4,'y'=4,'z'=16,'k'=2] {'x','y','k'}, dimensions={0} | all-to-all | bytes 524288 | tf_op jit(solution)/shard_map/all_to_all | solution.py:299
  201.5 14.6 %all_to_all.237.got_ref = bf16[16,8,512]{2,1,0:T(8,128)(2,1)S(1)} all-to-all(bf16[16,8,512]{2,1,0:T(8,128)(2,1)S(1)} %shard_map.88), channel_id=1, replica_groups=mesh['x'=4,'y'=4,'z'=16,'k'=2] {'z'}, dimensions={0} | all-to-all | bytes 262144 | tf_op jit(solution)/shard_map/all_to_all | solution.py:299
  216.2 3.8 %all-gather.1 = bf16[16,512]{1,0:T(8,128)(2,1)S(1)} all-gather(bf16[8,512]{1,0:T(8,128)(2,1)S(1)} %shard_map.89), channel_id=3, replica_groups=mesh['x'=4,'y'=4,'z'=16,'k'=2] {'k'}, dimensions={0}, use_global_device_ids=true | all-gather | bytes 24576 | tf_op jit(solution)/shard_map/all_gather | solution.py:302
  219.9 1.0 shard_map.90
  (16 shorter events, 3.2 us)
Async XLA Ops:
  0.6 19.6 %collective-permute-start = (bf16[1024,512]{1,0:T(8,128)(2,1)}, bf16[1024,512]{1,0:T(8,128)(2,1)S(1)}, u32[]{:S(2)}, u32[]{:S(2)}) collective-permute-start(bf16[1024,512]{1,0:T(8,128)(2,1)} %front_hbm.1), channel_id=1, source_target_pairs={{0,1},{1,0},{2,3},{3,2},{4,5},{5,4},{6,7},{7,6},{8,9},{9,8},{10,11... | collective-permute-start | bytes 3145736 | tf_op jit(solution)/shard_map/ppermute | solution.py:304
  20.3 168.0 %copy-start = (f32[1,1024]{1,0:T(1,128)S(1)}, f32[1,1024]{1,0:T(1,128)}, u32[]{:S(2)}) copy-start(f32[1,1024]{1,0:T(1,128)} %tie_ref.1) | copy-start | bytes 12292
  20.3 168.0 %copy-start.1 = (f32[1,1024]{1,0:T(1,128)S(1)}, f32[1,1024]{1,0:T(1,128)}, u32[]{:S(2)}) copy-start(f32[1,1024]{1,0:T(1,128)} %mass_ref.1) | copy-start | bytes 12292

commit v7 on v6

--- a/solution.py
+++ b/solution.py
@@ -203,8 +203,13 @@
     room, front_ref, partner_ref, got_ref, mine_ref, row_code_ref, col_code_ref, high_ref, low_ref, y_in_ref,
     modes_hbm, y_ref, x_ref, pending_ref, send_ref, modes_ref, sem,
 ):
-    modes_copy = pltpu.make_async_copy(modes_hbm, modes_ref, sem)
-    modes_copy.start()
+    size = modes_ref.shape[0] // sem.shape[0]
+    copies = [
+        pltpu.make_async_copy(modes_hbm.at[pl.ds(i * size, size)], modes_ref.at[pl.ds(i * size, size)], sem.at[i])
+        for i in range(sem.shape[0])
+    ]
+    for copy in copies:
+        copy.start()
     code = row_code_ref[...]
     level = LEVELS - 1
     chosen = in_level(code, level, 8)
@@ -216,7 +221,8 @@
     out = back_product(x, front_ref, partner_ref)
     pending_ref[...] = out
     send_to_all(send_ref, pick(out, col_code_ref[...], (level - 1) * 8, room))
-    modes_copy.wait()
+    for copy in copies:
+        copy.wait()
 
 
 def back_kernel(level, room, got_ref, col_code_ref, high_ref, low_ref, y_ref, send_ref):
@@ -338,7 +344,7 @@
         y, x, pending, send, mode_rows = call(
             bound(turn_kernel, room), [flat, flat, flat, slots, (mode_shape, BF16)],
             front, partner, got, mine, row_code, col_code, high, low, y, Far(mode_rows),
-            scratch=[pltpu.SemaphoreType.DMA(())],
+            scratch=[pltpu.SemaphoreType.DMA((4,))],
         )
         for level in reversed(range(LEVELS - 1)):
             (send,) = call(

time: 223 us -> 227 us (1.018)
  blocking collectives: 202 us -> 205 us
    all_to_all x14, blocking collectives: 181 us -> 184 us  [exchange(): return lax.all_to_all(value, axes, 0, 0, tiled=True)]
where the time goes in v7:
time: 227 us; the launch traced here: 225 us
  blocking collectives  205 us (90%)
  Pallas kernels  9.84 us (4%)
  starting transfers between devices  8.75 us (4%)
    all_to_all x14, blocking collectives, exchange(): return lax.all_to_all(value, axes, 0, 0, tiled=True)  184 us
    all_gather x2, blocking collectives, both_cores(): return lax.all_gather(value, 'k', axis=0)  21.2 us
    pallas_call x17, Pallas kernels, call(): pl.pallas_call(body, out_shape=[pltpu.VMEM(*out) if isinstance(out, tuple...  9.84 us
    ppermute x1, starting transfers between devices, on_device(): lax.ppermute(front, 'k', [(core, 1 - core) for core in range(cores)])  8.75 us
  transfers between devices with their start and end apart: 1, of which 0 were waited for; matrix products, arithmetic and copies ran while one was open for 0% of the time, Pallas kernels for 1%

profile of v7, /device:TPU:1, one launch (start us, length us, event | category | flops | bytes accessed | tf_op | source)
XLA Modules:
  0.0 224.5 jit_solution(4837028776528033639)
XLA Ops:
  0.6 8.7 %collective-permute-start = (bf16[1024,512]{1,0:T(8,128)(2,1)}, bf16[1024,512]{1,0:T(8,128)(2,1)S(1)}, u32[]{:S(2)}, u32[]{:S(2)}) collective-permute-start(bf16[1024,512]{1,0:T(8,128)(2,1)} %front_hbm.1), channel_id=1, source_target_pairs={{0,1},{1,0},{2,3},{3,2},{4,5},{5,4},{6,7},{7,6},{8,9},{9,8},{10,11... | collective-permute-start | bytes 3145736 | tf_op jit(solution)/shard_map/ppermute | solution.py:310
  9.4 1.5 shard_map.86
  10.9 9.3 %all_to_all.235 = bf16[16,4,1024]{2,1,0:T(4,128)(2,1)S(1)} all-to-all(bf16[16,4,1024]{2,1,0:T(4,128)(2,1)S(1)} %get-tuple-element.210), channel_id=1, replica_groups=mesh['x'=4,'y'=4,'z'=16,'k'=2] {'x','y'}, dimensions={0} | all-to-all | bytes 262144 | tf_op jit(solution)/shard_map/all_to_all | solution.py:305
  20.3 153.9 %conditional.1 = (f32[4,1024]{1,0:T(4,128)S(1)}, bf16[1024,1024]{1,0:T(8,128)(2,1)S(1)}) conditional(s32[]{:T(128)} %bitcast.1, (bf16[1024,512]{1,0:T(8,128)(2,1)S(1)}, bf16[1024,512]{1,0:T(8,128)(2,1)S(1)}, bf16[16,4,1024]{2,1,0:T(4,128)(2,1)S(1)}, s32[4,1024]{1,0:T(4,128)S(1)}, s32[4,1024]{1,0:T(4,128)S(1)}, ...), branch_computations={%region_0.0_spmd, %region_1.0_spmd, %region_2.0_spmd, %region_3.0_... | conditional | bytes 2883600 | solution.py:366
  20.3 0.7 branch_1_fun.12
  21.0 25.1 %all_to_all.202.refs_0_ = bf16[16,4,640]{2,1,0:T(4,128)(2,1)S(1)} all-to-all(bf16[16,4,640]{2,1,0:T(4,128)(2,1)S(1)} %get-tuple-element.113), channel_id=1, replica_groups=mesh['x'=4,'y'=4,'z'=16,'k'=2] {'z'}, dimensions={0} | all-to-all | bytes 163840 | tf_op jit(solution)/shard_map/cond/branch_1_fun/all_to_all | solution.py:305
  46.5 9.9 %all_to_all.203.refs_2_ = bf16[16,4,640]{2,1,0:T(4,128)(2,1)S(1)} all-to-all(bf16[16,4,640]{2,1,0:T(4,128)(2,1)S(1)} %get-tuple-element.118), channel_id=1, replica_groups=mesh['x'=4,'y'=4,'z'=16,'k'=2] {'x','y'}, dimensions={0} | all-to-all | bytes 163840 | tf_op jit(solution)/shard_map/cond/branch_1_fun/all_to_all | solution.py:305
  56.4 0.7 branch_1_fun.14
  57.1 14.8 %all_to_all.204.refs_0_ = bf16[16,4,640]{2,1,0:T(4,128)(2,1)S(1)} all-to-all(bf16[16,4,640]{2,1,0:T(4,128)(2,1)S(1)} %get-tuple-element.120), channel_id=1, replica_groups=mesh['x'=4,'y'=4,'z'=16,'k'=2] {'z'}, dimensions={0} | all-to-all | bytes 163840 | tf_op jit(solution)/shard_map/cond/branch_1_fun/all_to_all | solution.py:305
  72.3 9.8 %all_to_all.205.refs_2_ = bf16[16,4,640]{2,1,0:T(4,128)(2,1)S(1)} all-to-all(bf16[16,4,640]{2,1,0:T(4,128)(2,1)S(1)} %get-tuple-element.122), channel_id=1, replica_groups=mesh['x'=4,'y'=4,'z'=16,'k'=2] {'x','y'}, dimensions={0} | all-to-all | bytes 163840 | tf_op jit(solution)/shard_map/cond/branch_1_fun/all_to_all | solution.py:305
  82.1 0.7 branch_1_fun.16
  82.7 14.8 %all_to_all.206.refs_2_ = bf16[16,4,640]{2,1,0:T(4,128)(2,1)S(1)} all-to-all(bf16[16,4,640]{2,1,0:T(4,128)(2,1)S(1)} %branch_1_fun.16), channel_id=1, replica_groups=mesh['x'=4,'y'=4,'z'=16,'k'=2] {'z'}, dimensions={0} | all-to-all | bytes 163840 | tf_op jit(solution)/shard_map/cond/branch_1_fun/all_to_all | solution.py:305
  97.5 2.1 branch_1_fun.17
  99.6 9.5 %all_to_all.207.refs_0_ = bf16[16,4,640]{2,1,0:T(4,128)(2,1)S(1)} all-to-all(bf16[16,4,640]{2,1,0:T(4,128)(2,1)S(1)} %get-tuple-element.126), channel_id=1, replica_groups=mesh['x'=4,'y'=4,'z'=16,'k'=2] {'x','y'}, dimensions={0} | all-to-all | bytes 163840 | tf_op jit(solution)/shard_map/cond/branch_1_fun/all_to_all | solution.py:305
  109.5 14.7 %all_to_all.208.refs_2_ = bf16[16,4,640]{2,1,0:T(4,128)(2,1)S(1)} all-to-all(bf16[16,4,640]{2,1,0:T(4,128)(2,1)S(1)} %branch_1_fun.18), channel_id=1, replica_groups=mesh['x'=4,'y'=4,'z'=16,'k'=2] {'z'}, dimensions={0} | all-to-all | bytes 163840 | tf_op jit(solution)/shard_map/cond/branch_1_fun/all_to_all | solution.py:305
  124.6 9.5 %all_to_all.209.refs_0_ = bf16[16,4,640]{2,1,0:T(4,128)(2,1)S(1)} all-to-all(bf16[16,4,640]{2,1,0:T(4,128)(2,1)S(1)} %get-tuple-element.130), channel_id=1, replica_groups=mesh['x'=4,'y'=4,'z'=16,'k'=2] {'x','y'}, dimensions={0} | all-to-all | bytes 163840 | tf_op jit(solution)/shard_map/cond/branch_1_fun/all_to_all | solution.py:305
  134.4 14.5 %all_to_all.210.refs_2_ = bf16[16,4,640]{2,1,0:T(4,128)(2,1)S(1)} all-to-all(bf16[16,4,640]{2,1,0:T(4,128)(2,1)S(1)} %branch_1_fun.20), channel_id=1, replica_groups=mesh['x'=4,'y'=4,'z'=16,'k'=2] {'z'}, dimensions={0} | all-to-all | bytes 163840 | tf_op jit(solution)/shard_map/cond/branch_1_fun/all_to_all | solution.py:305
  149.3 9.8 %all_to_all.211.refs_0_ = bf16[16,4,640]{2,1,0:T(4,128)(2,1)S(1)} all-to-all(bf16[16,4,640]{2,1,0:T(4,128)(2,1)S(1)} %get-tuple-element.133), channel_id=1, replica_groups=mesh['x'=4,'y'=4,'z'=16,'k'=2] {'x','y'}, dimensions={0} | all-to-all | bytes 163840 | tf_op jit(solution)/shard_map/cond/branch_1_fun/all_to_all | solution.py:305
  159.4 14.5 %all_to_all.212.refs_0_ = bf16[16,4,640]{2,1,0:T(4,128)(2,1)S(1)} all-to-all(bf16[16,4,640]{2,1,0:T(4,128)(2,1)S(1)} %branch_1_fun.22), channel_id=1, replica_groups=mesh['x'=4,'y'=4,'z'=16,'k'=2] {'z'}, dimensions={0} | all-to-all | bytes 163840 | tf_op jit(solution)/shard_map/cond/branch_1_fun/all_to_all | solution.py:305
  174.1 16.9 %all-gather.2.pair_ref = f32[2,4,1024]{2,1,0:T(4,128)S(1)} all-gather(f32[1,4,1024]{2,1,0:T(4,128)S(1)} %bitcast.6), channel_id=2, replica_groups=mesh['x'=4,'y'=4,'z'=16,'k'=2] {'k'}, dimensions={0}, use_global_device_ids=true | all-gather | bytes 49152 | tf_op jit(solution)/shard_map/all_gather | solution.py:308
  191.7 12.6 %all_to_all.236.got_ref = bf16[32,8,512]{2,1,0:T(8,128)(2,1)S(1)} all-to-all(bf16[32,8,512]{2,1,0:T(8,128)(2,1)S(1)} %get-tuple-element.224), channel_id=1, replica_groups=mesh['x'=4,'y'=4,'z'=16,'k'=2] {'x','y','k'}, dimensions={0} | all-to-all | bytes 524288 | tf_op jit(solution)/shard_map/all_to_all | solution.py:305
  204.4 14.8 %all_to_all.237.got_ref = bf16[16,8,512]{2,1,0:T(8,128)(2,1)S(1)} all-to-all(bf16[16,8,512]{2,1,0:T(8,128)(2,1)S(1)} %shard_map.88), channel_id=1, replica_groups=mesh['x'=4,'y'=4,'z'=16,'k'=2] {'z'}, dimensions={0} | all-to-all | bytes 262144 | tf_op jit(solution)/shard_map/all_to_all | solution.py:305
  219.2 4.3 %all-gather.1 = bf16[16,512]{1,0:T(8,128)(2,1)S(1)} all-gather(bf16[8,512]{1,0:T(8,128)(2,1)S(1)} %shard_map.89), channel_id=3, replica_groups=mesh['x'=4,'y'=4,'z'=16,'k'=2] {'k'}, dimensions={0}, use_global_device_ids=true | all-gather | bytes 24576 | tf_op jit(solution)/shard_map/all_gather | solution.py:308
  223.5 1.0 shard_map.90
  (16 shorter events, 3.2 us)
Async XLA Ops:
  0.6 19.6 %collective-permute-start = (bf16[1024,512]{1,0:T(8,128)(2,1)}, bf16[1024,512]{1,0:T(8,128)(2,1)S(1)}, u32[]{:S(2)}, u32[]{:S(2)}) collective-permute-start(bf16[1024,512]{1,0:T(8,128)(2,1)} %front_hbm.1), channel_id=1, source_target_pairs={{0,1},{1,0},{2,3},{3,2},{4,5},{5,4},{6,7},{7,6},{8,9},{9,8},{10,11... | collective-permute-start | bytes 3145736 | tf_op jit(solution)/shard_map/ppermute | solution.py:310
  20.3 170.8 %copy-start = (f32[1,1024]{1,0:T(1,128)S(1)}, f32[1,1024]{1,0:T(1,128)}, u32[]{:S(2)}) copy-start(f32[1,1024]{1,0:T(1,128)} %tie_ref.1) | copy-start | bytes 12292
  20.3 170.8 %copy-start.1 = (f32[1,1024]{1,0:T(1,128)S(1)}, f32[1,1024]{1,0:T(1,128)}, u32[]{:S(2)}) copy-start(f32[1,1024]{1,0:T(1,128)} %mass_ref.1) | copy-start | bytes 12292
